TPU v7x, 32 devices: a whole 2x2x4 slice. The times are simulated.
32 devices in a mesh: dp: 8 (over z, x), seq: 4 (over y, core).
Axes of the slice: x: 2, y: 2, z: 4, core: 2. Of those that a mesh axis runs over, the one named last changes fastest.
Arguments:
- tokens: bfloat16 [24, 512, 768], P('dp', 'seq'), may hold values from -6 to 6
- segment_ids: int32 [24, 512], P('dp'), may hold values from 0 to 7, never falling along the last dimension, each value on 1 to 128 neighbouring positions
- padding: int32 [24, 512], P('dp'), may hold values 0 or 1
- clusters: int32 [24, 12, 512], P('dp'), may hold values from 0 to 511, as said below
- w_query: bfloat16 [768, 768], replicated, may hold values from -0.4375 to 0.4375
- w_key: bfloat16 [768, 768], replicated, may hold values from -0.21875 to 0.21875
- w_value: bfloat16 [768, 768], replicated, may hold values from -0.21875 to 0.21875
- w_output: bfloat16 [768, 768], replicated, may hold values from -0.875 to 0.875
- b_query: bfloat16 [768], replicated, may hold values from -4 to 4
- b_value: bfloat16 [768], replicated, may hold values from -4 to 4
- b_output: bfloat16 [768], replicated, may hold values from -4 to 4
- gain_attn: bfloat16 [768], replicated, may hold values from 0.5 to 1.5
- shift_attn: bfloat16 [768], replicated, may hold values from -4 to 4
- w_inner: bfloat16 [768, 3072], P(None, 'seq'), may hold values from -0.21875 to 0.21875
- b_inner: bfloat16 [3072], P('seq'), may hold values from -4 to 4
- w_outer: bfloat16 [3072, 768], P('seq'), may hold values from -0.15625 to 0.15625
- b_outer: bfloat16 [768], replicated, may hold values from -4 to 4
- gain_ffn: bfloat16 [768], replicated, may hold values from 0.5 to 1.5
- shift_ffn: bfloat16 [768], replicated, may hold values from -4 to 4
- cotangent: bfloat16 [24, 512, 768], P('dp', 'seq'), may hold values from -6 to 6
Outputs:
- output: bfloat16 [24, 512, 768], P('dp', 'seq')
- grad_tokens: bfloat16 [24, 512, 768], P('dp', 'seq')
- grad_w_query: float32 [768, 768], replicated
- grad_w_key: float32 [768, 768], replicated
- grad_w_value: float32 [768, 768], replicated
- grad_w_output: float32 [768, 768], replicated
- grad_b_query: float32 [768], replicated
- grad_b_value: float32 [768], replicated
- grad_b_output: float32 [768], replicated
- grad_gain_attn: float32 [768], replicated
- grad_shift_attn: float32 [768], replicated
- grad_w_inner: float32 [768, 3072], P(None, 'seq')
- grad_b_inner: float32 [3072], P('seq')
- grad_w_outer: float32 [3072, 768], P('seq')
- grad_b_outer: float32 [768], replicated
- grad_gain_ffn: float32 [768], replicated
- grad_shift_ffn: float32 [768], replicated
- cluster_log: float32 [2, 12], replicated
Inputs may be any that keep to these rules, and one draw needn't show every extreme that they name: For each row and head, clusters lists every position of the row once; each cluster of 128 consecutive entries takes at most 64 positions from each run of positions k * 128 to (k + 1) * 128 - 1, and in every row some head has a cluster that takes exactly 64 from one run.
All inputs are finite; a program needn't handle non-finite values. No bound on the sum of `padding` on one device may be relied on, other than what follows from the above.
Results may differ from a plain program's by a relative error of at most 0.018.
The roundings to bfloat16 on the way count: a program that leaves them out, or rounds other values in their place, can miss the bound.
Values may be sent and summed in bfloat16 or wider, within the bound.
No kernel may reach another device: no remote copies, remote signals or barrier semaphores. Data moves between devices by JAX's collectives and lax.ppermute only.
A program may use at most 192 MiB of HBM per device.

v0:
```python
import jax
import jax.numpy as jnp
from jax import lax
from jax.experimental import pallas as pl
from jax.experimental.pallas import tpu as pltpu
from jax.sharding import PartitionSpec as P


EPSILON = 1e-12
NEGATIVE = -1e30
LANES = 128
AXES = ("dp", "seq")
F32 = jnp.float32
BF16 = jnp.bfloat16


def dot_nn(left, right):
    return lax.dot_general(left, right, (((1,), (0,)), ((), ())), preferred_element_type=F32)


def dot_nt(left, right):
    return lax.dot_general(left, right, (((1,), (1,)), ((), ())), preferred_element_type=F32)


def dot_tn(left, right):
    return lax.dot_general(left, right, (((0,), (0,)), ((), ())), preferred_element_type=F32)


def codes_kernel(where_ref, cl_ref, seg_ref, pad_ref, qrow_ref, krow_ref, qcol_ref, kcol_ref):
    row = pl.program_id(0)
    head_count = cl_ref.shape[1]
    length = cl_ref.shape[2]
    spot = lax.broadcasted_iota(jnp.int32, (LANES, length), 0)
    line = lax.broadcasted_iota(jnp.int32, (8, length), 0)
    cluster = lax.broadcasted_iota(jnp.int32, (8, length), 1) // LANES
    anchors = [where_ref[0], where_ref[1], where_ref[2]]
    edge_ok = where_ref[3] == 1
    want = jnp.where(line == 0, anchors[0], jnp.where(line == 1, anchors[1], anchors[2]))
    want = jnp.where(line < 3, want, -1)
    qrow_ref[...] = jnp.full(qrow_ref.shape, -2.0, F32)
    krow_ref[...] = jnp.full(krow_ref.shape, -1.0, F32)
    segs, pads = [], []
    for block in range(3):
        start = pl.multiple_of(anchors[block] * LANES, LANES)
        segs.append(row_of(seg_ref[:, pl.ds(start, LANES)], row).astype(F32))
        pads.append(row_of(pad_ref[:, pl.ds(start, LANES)], row))
    for head in range(head_count):
        members = cl_ref[0, head : head + 1, :]
        onehot = (spot == (members % LANES)).astype(F32).astype(BF16)
        chosen = jnp.where((members // LANES) == want, cluster, 0).astype(F32).astype(BF16)
        found = dot_nt(chosen, onehot)
        for block in range(3):
            code = found[block : block + 1, :] * 8.0 + segs[block]
            query, key = code, jnp.where(pads[block] == 1, code, -1.0)
            if block == 2:
                query = jnp.where(edge_ok, query, -2.0)
                key = jnp.where(edge_ok, key, -1.0)
            at = block * 16 + head
            qrow_ref[0, at : at + 1, :] = query
            krow_ref[0, at : at + 1, :] = key
    qrow_ref[0, 48:49, :] = (pads[0] == 1).astype(F32)
    qcol_ref[0] = qrow_ref[0].T
    kcol_ref[0] = krow_ref[0].T


def row_of(block, row):
    chosen = lax.broadcasted_iota(jnp.int32, block.shape, 0) == row
    return jnp.sum(jnp.where(chosen, block, 0), axis=0, keepdims=True)


def cluster_codes(clusters, segment_ids, padding, where_at):
    row_count, head_count, length = clusters.shape
    table = jax.ShapeDtypeStruct((row_count, LANES, LANES), F32)
    spec = pl.BlockSpec((1, LANES, LANES), lambda r, w: (r, 0, 0))
    return pl.pallas_call(
        codes_kernel,
        out_shape=(table,) * 4,
        grid_spec=pltpu.PrefetchScalarGridSpec(
            num_scalar_prefetch=1,
            grid=(row_count,),
            in_specs=[
                pl.BlockSpec((1, head_count, length), lambda r, w: (r, 0, 0)),
                pl.BlockSpec((row_count, length), lambda r, w: (0, 0)),
                pl.BlockSpec((row_count, length), lambda r, w: (0, 0)),
            ],
            out_specs=[spec] * 4,
        ),
        name="codes",
    )(where_at, clusters, segment_ids, padding)


def widen_kernel(*refs):
    for index, ref in enumerate(refs[:-1]):
        refs[-1][index : index + 1, :] = ref[...].astype(F32).reshape(1, ref.shape[0])


def widened(vectors):
    return pl.pallas_call(
        widen_kernel, out_shape=jax.ShapeDtypeStruct((len(vectors),) + vectors[0].shape, F32), name="widen"
    )(*vectors)


def halves(value):
    low = lax.broadcasted_iota(jnp.int32, value.shape, 1) < (LANES // 2)
    zero = jnp.zeros_like(value)
    return jnp.where(low, value, zero), jnp.where(low, zero, value)


def pick(even, odd):
    return jnp.where(lax.broadcasted_iota(jnp.int32, even.shape, 1) < (LANES // 2), even, odd)


def diagonal():
    return lax.broadcasted_iota(jnp.int32, (LANES, LANES), 0) == lax.broadcasted_iota(
        jnp.int32, (LANES, LANES), 1
    )


def attend_kernel(
    model, q_ref, k_ref, v_ref, kc_ref, ke_ref, vc_ref, ve_ref, krow_ref, qcol_ref, ctx_ref, lse_ref, stat_ref
):
    eye = diagonal()
    lane = lax.broadcasted_iota(jnp.int32, (LANES, LANES), 1)
    lse_all = jnp.zeros((LANES, LANES), F32)
    entropy_all = jnp.zeros((LANES, LANES), F32)
    count_all = jnp.ones((LANES, LANES), F32)
    for pair in range(model // LANES):
        at = slice(pair * LANES, (pair + 1) * LANES)
        queries = halves(q_ref[0, :, at])
        keys = jnp.concatenate([r[0, :, at] for r in (k_ref, kc_ref, ke_ref)], axis=0)
        values = jnp.concatenate([r[0, :, at] for r in (v_ref, vc_ref, ve_ref)], axis=0)
        out = []
        for side in range(2):
            head = pair * 2 + side
            raw = dot_nt(queries[side], keys)
            code = qcol_ref[0, :, head : head + 1]
            allowed = [code == krow_ref[0, b * 16 + head : b * 16 + head + 1, :] for b in range(3)]
            allowed[0] = allowed[0] | eye
            allowed = jnp.concatenate(allowed, axis=1)
            masked = jnp.where(allowed, raw, NEGATIVE)
            top = jnp.max(masked, axis=1, keepdims=True)
            grown = jnp.exp(masked - top)
            total = jnp.sum(grown, axis=1, keepdims=True)
            prob = grown * (1.0 / total)
            lse = top + jnp.log(total)
            entropy = lse - jnp.sum(prob * masked, axis=1, keepdims=True)
            count = jnp.sum(jnp.where(allowed, 1.0, 0.0), axis=1, keepdims=True)
            out.append(dot_nn(prob.astype(BF16), values))
            lse_all = jnp.where(lane == head, lse, lse_all)
            entropy_all = jnp.where(lane == head, entropy, entropy_all)
            count_all = jnp.where(lane == head, count, count_all)
        ctx_ref[0, :, at] = pick(out[0], out[1]).astype(BF16)
    real = qcol_ref[0, :, 48:49]
    stat_ref[0] = jnp.zeros(stat_ref.shape[1:], F32)
    stat_ref[0, 0:1, :] = jnp.sum(entropy_all * real, axis=0, keepdims=True)
    stat_ref[0, 1:2, :] = jnp.sum(jnp.log(count_all) * real, axis=0, keepdims=True)
    stat_ref[0, 2:3, :] = jnp.sum(jnp.broadcast_to(real, (LANES, LANES)), axis=0, keepdims=True)
    lse_ref[0] = lse_all.T[:16, :]


def attend(q, k, v, kc, ke, vc, ve, krow, qcol):
    row_count, shard_len, model = q.shape
    own = pl.BlockSpec((1, shard_len, model), lambda r: (r, 0, 0))
    table = pl.BlockSpec((1, LANES, LANES), lambda r: (r, 0, 0))
    return pl.pallas_call(
        lambda *refs: attend_kernel(model, *refs),
        out_shape=(
            jax.ShapeDtypeStruct(q.shape, BF16),
            jax.ShapeDtypeStruct((row_count, 16, LANES), F32),
            jax.ShapeDtypeStruct((row_count, 8, LANES), F32),
        ),
        grid=(row_count,),
        in_specs=[own] * 7 + [table] * 2,
        out_specs=(
            own,
            pl.BlockSpec((1, 16, LANES), lambda r: (r, 0, 0)),
            pl.BlockSpec((1, 8, LANES), lambda r: (r, 0, 0)),
        ),
        name="attend",
    )(q, k, v, kc, ke, vc, ve, krow, qcol)


def pull_query_kernel(
    model, q_ref, k_ref, v_ref, d_ref, kc_ref, ke_ref, vc_ref, ve_ref, row_ref, krow_ref, qcol_ref, out_ref, bias_ref
):
    eye = diagonal()
    cols = jnp.concatenate([row_ref[0], jnp.zeros((LANES - 32, LANES), F32)], axis=0).T
    bias_ref[0] = jnp.zeros(bias_ref.shape[1:], F32)
    for pair in range(model // LANES):
        at = slice(pair * LANES, (pair + 1) * LANES)
        queries, grads = halves(q_ref[0, :, at]), halves(d_ref[0, :, at])
        k_all = jnp.concatenate([r[0, :, at] for r in (k_ref, kc_ref, ke_ref)], axis=0)
        v_all = jnp.concatenate([r[0, :, at] for r in (v_ref, vc_ref, ve_ref)], axis=0)
        dq = []
        for side in range(2):
            head = pair * 2 + side
            code = qcol_ref[0, :, head : head + 1]
            allowed = [code == krow_ref[0, b * 16 + head : b * 16 + head + 1, :] for b in range(3)]
            allowed[0] = allowed[0] | eye
            raw = dot_nt(queries[side], k_all)
            lse, delta = cols[:, head : head + 1], cols[:, 16 + head : 17 + head]
            prob = jnp.exp(jnp.where(jnp.concatenate(allowed, axis=1), raw, NEGATIVE) - lse)
            d_score = (prob * (dot_nt(grads[side], v_all) - delta)).astype(BF16)
            dq.append(dot_nn(d_score, k_all))
        low = pick(dq[0], dq[1]).astype(BF16)
        wide = low.astype(F32) * 0.125
        out_ref[0, :, at] = wide.astype(BF16)
        bias_ref[0, 0:1, at] = jnp.sum(wide, axis=0, keepdims=True)


def pull_pair_kernel(
    model,
    q_ref,
    k_ref,
    v_ref,
    d_ref,
    qc_ref,
    qe_ref,
    dc_ref,
    de_ref,
    row_ref,
    rowc_ref,
    rowe_ref,
    qrow_ref,
    kcol_ref,
    out_ref,
    bias_ref,
):
    eye = diagonal()
    bias_ref[0] = jnp.zeros(bias_ref.shape[1:], F32)
    for pair in range(model // LANES):
        at = slice(pair * LANES, (pair + 1) * LANES)
        keys, values = halves(k_ref[0, :, at]), halves(v_ref[0, :, at])
        q_all = jnp.concatenate([r[0, :, at] for r in (q_ref, qc_ref, qe_ref)], axis=0)
        d_all = jnp.concatenate([r[0, :, at] for r in (d_ref, dc_ref, de_ref)], axis=0)
        dk, dv = [], []
        for side in range(2):
            head = pair * 2 + side
            code = kcol_ref[0, :, head : head + 1]
            allowed = [code == qrow_ref[0, b * 16 + head : b * 16 + head + 1, :] for b in range(3)]
            allowed[0] = allowed[0] | eye
            raw = dot_nt(keys[side], q_all)
            lse = jnp.concatenate([r[0, head : head + 1, :] for r in (row_ref, rowc_ref, rowe_ref)], axis=1)
            delta = jnp.concatenate(
                [r[0, 16 + head : 17 + head, :] for r in (row_ref, rowc_ref, rowe_ref)], axis=1
            )
            prob = jnp.exp(jnp.where(jnp.concatenate(allowed, axis=1), raw, NEGATIVE) - lse)
            d_score = (prob * (dot_nt(values[side], d_all) - delta)).astype(BF16)
            dk.append(dot_nn(d_score, q_all))
            dv.append(dot_nn(prob.astype(BF16), d_all))
        for index, both in enumerate((dk, dv)):
            low = pick(both[0], both[1]).astype(BF16)
            spot = slice(index * model + pair * LANES, index * model + (pair + 1) * LANES)
            out_ref[0, :, spot] = low
            bias_ref[0, 0:1, spot] = jnp.sum(low.astype(F32), axis=0, keepdims=True)


def pull(kernel, copies, activations, lines, tables):
    row_count, shard_len, model = activations[0].shape
    own = pl.BlockSpec((1, shard_len, model), lambda r: (r, 0, 0))
    table = pl.BlockSpec((1, LANES, LANES), lambda r: (r, 0, 0))
    line = pl.BlockSpec((1, 32, LANES), lambda r: (r, 0, 0))
    return pl.pallas_call(
        lambda *refs: kernel(model, *refs),
        out_shape=(
            jax.ShapeDtypeStruct((row_count, shard_len, copies * model), BF16),
            jax.ShapeDtypeStruct((row_count, 8, copies * model), F32),
        ),
        grid=(row_count,),
        in_specs=[own] * len(activations) + [line] * len(lines) + [table] * len(tables),
        out_specs=(
            pl.BlockSpec((1, shard_len, copies * model), lambda r: (r, 0, 0)),
            pl.BlockSpec((1, 8, copies * model), lambda r: (r, 0, 0)),
        ),
    )(*activations, *lines, *tables)


def normed(value):
    centred = value - jnp.mean(value, axis=-1, keepdims=True)
    inverse = lax.rsqrt(jnp.mean(centred * centred, axis=-1, keepdims=True) + EPSILON)
    return centred * inverse, inverse


def norm_pull(grad, gain, unit, inverse):
    scaled = grad * gain
    moved = scaled - jnp.mean(scaled, axis=-1, keepdims=True)
    moved = moved - unit * jnp.mean(scaled * unit, axis=-1, keepdims=True)
    return moved * inverse


def gelu_both(value):
    cdf = 0.5 * (1.0 + lax.erf(value * (0.5**0.5)))
    density = jnp.exp(-0.5 * value * value) * 0.3989422804014327
    return value * cdf, cdf + value * density


class Links:
    def __init__(self, dp_size, seq_size):
        self.dp, self.seq = dp_size, seq_size
        self.dp_at, self.seq_at = lax.axis_index("dp"), lax.axis_index("seq")
        self.bits = [1 << n for n in range(1, dp_size.bit_length() - 1)]

    def swap(self, value, dp_bits, seq_bits):
        pairs = [
            (d * self.seq + s, (d ^ dp_bits) * self.seq + (s ^ seq_bits))
            for d in range(self.dp)
            for s in range(self.seq)
        ]
        return lax.ppermute(value, AXES, pairs)

    def edge(self, value):
        pairs = []
        for d in range(self.dp):
            for s in range(1, self.seq - 1, 2):
                pairs.append((d * self.seq + s, d * self.seq + s + 1))
                pairs.append((d * self.seq + s + 1, d * self.seq + s))
        return lax.ppermute(value, AXES, pairs)

    def dp_stage(self, bit):
        return [(0, 0), (bit, 0)], (self.dp_at // bit) % 2, "x" if bit == 1 else "z%d" % bit

    def y_stage(self):
        return [(0, 0), (0, 2)], self.seq_at // 2, "y"

    def plane(self):
        return [(j & 1, (j >> 1) * 2) for j in range(4)], (self.dp_at % 2) + 2 * (self.seq_at // 2), "p"

    def z_stages(self):
        return [self.dp_stage(bit) for bit in self.bits]

    def wide_z_stages(self):
        stages, stride = [], 2
        while stride < self.dp:
            radix = min(4, self.dp // stride)
            partners = [(j * stride, 0) for j in range(radix)]
            stages.append((partners, (self.dp_at // stride) % radix, "w%d" % stride))
            stride *= radix
        return stages

    def spread(self, value, stage, axis=0):
        partners, mine, _ = stage
        rows = value.shape[axis] // len(partners)
        total = lax.dynamic_slice_in_dim(value, mine * rows, rows, axis).astype(F32)
        for index in range(1, len(partners)):
            sent = lax.dynamic_slice_in_dim(value, (mine ^ index) * rows, rows, axis)
            total = total + self.swap(sent, *partners[index]).astype(F32)
        return total.astype(BF16)

    def collect(self, value, stage, axis=0):
        partners, mine, _ = stage
        pieces = [value]
        for index in range(1, len(partners)):
            pieces.append(self.swap(value, *partners[index]))
        bit = 1
        while bit < len(pieces):
            odd = (mine // bit) % 2 == 1
            pieces = [jnp.where(odd, pieces[n ^ bit], pieces[n]) for n in range(len(pieces))]
            bit *= 2
        return jnp.concatenate(pieces, axis=axis)

    def core_spread(self, value):
        mine = self.seq_at % 2
        cols = value.shape[1] // 2
        keep = lax.dynamic_slice_in_dim(value, mine * cols, cols, 1)
        sent = lax.dynamic_slice_in_dim(value, (1 - mine) * cols, cols, 1)
        return (keep.astype(F32) + self.swap(sent, 0, 1).astype(F32)).astype(BF16)

    def core_collect(self, value):
        mine = self.seq_at % 2
        other = self.swap(value, 0, 1)
        return jnp.where(mine == 0, value, other), jnp.where(mine == 0, other, value)

    def total(self, value):
        for bits in (1, 2):
            value = value + self.swap(value, 0, bits)
        stride = 1
        while stride < self.dp:
            value = value + self.swap(value, stride, 0)
            stride *= 2
        return value

    def around(self, value, stages, axis=0):
        for stage in stages:
            value = self.spread(value, stage, axis)
        for stage in reversed(stages):
            value = self.collect(value, stage, axis)
        return value


def body(
    tokens,
    segment_ids,
    padding,
    clusters,
    w_query,
    w_key,
    w_value,
    w_output,
    b_query,
    b_value,
    b_output,
    gain_attn,
    shift_attn,
    w_inner,
    b_inner,
    w_outer,
    b_outer,
    gain_ffn,
    shift_ffn,
    cotangent,
):
    links = Links(lax.axis_size("dp"), lax.axis_size("seq"))
    seq_at, seq_count = links.seq_at, links.seq
    row_count, shard_len, model = tokens.shape
    head_count = clusters.shape[1]
    amount = row_count * shard_len
    own_shape = (row_count, shard_len, model)
    tokens_edge = links.edge(tokens)
    tokens_core = links.swap(tokens, 0, 1)
    inner, outer, inner_bias = [w_inner], [w_outer], [b_inner[None, :]]
    inner.append(links.swap(w_inner, 0, 2))
    outer.append(links.swap(w_outer, 0, 2))
    inner_bias.append(links.swap(inner_bias[0], 0, 2))
    for index in range(2):
        inner.append(links.swap(inner[index], 0, 1))
        outer.append(links.swap(outer[index], 0, 1))
    both = links.swap(jnp.concatenate(inner_bias, axis=0), 0, 1)
    inner_bias += [both[0:1], both[1:2]]

    line = lax.broadcasted_iota(jnp.int32, (4,), 0)
    edge_raw = jnp.where(seq_at % 2 == 1, seq_at + 1, seq_at - 1)
    edge_ok = (edge_raw >= 0) & (edge_raw < seq_count)
    where_at = jnp.where(line == 2, jnp.clip(edge_raw, 0, seq_count - 1), edge_ok.astype(jnp.int32))
    where_at = jnp.where(line == 0, seq_at, jnp.where(line == 1, seq_at ^ 1, where_at)).astype(jnp.int32)
    qrow, krow, qcol, kcol = cluster_codes(clusters, segment_ids, padding, where_at)
    vectors = [b_query, b_value, b_output, gain_attn, shift_attn, b_outer, gain_ffn, shift_ffn]
    vectors = widened(vectors)
    bias_query, bias_value, bias_output, gain_one, shift_one, bias_outer, gain_two, shift_two = [
        vectors[n : n + 1] for n in range(8)
    ]

    def make_query(array):
        return ((dot_nn(array, w_query) + bias_query) * 0.125).astype(BF16).reshape(own_shape)

    def make_key(array):
        return dot_nn(array, w_key).astype(BF16).reshape(own_shape)

    def make_value(array):
        return (dot_nn(array, w_value) + bias_value).astype(BF16).reshape(own_shape)

    flat = tokens.reshape(amount, model)
    flat_core, flat_edge = tokens_core.reshape(amount, model), tokens_edge.reshape(amount, model)
    q, k, v = make_query(flat), make_key(flat), make_value(flat)
    k_core, v_core = make_key(flat_core), make_value(flat_core)
    k_edge, v_edge = make_key(flat_edge), make_value(flat_edge)
    context, lse, stats = attend(q, k, v, k_core, k_edge, v_core, v_edge, krow, qcol)
    q_core, q_edge = make_query(flat_core), make_query(flat_edge)
    context = context.reshape(amount, model)

    x = flat.astype(F32)
    residual_one = x + dot_nn(context, w_output) + bias_output
    unit_one, inverse_one = normed(residual_one)
    mid = unit_one * gain_one + shift_one
    mid_low = mid.astype(BF16)

    acts, slopes = [None] * 4, [None] * 4
    residual_two = mid + bias_outer
    for index in (0, 2, 1, 3):
        pre = dot_nn(mid_low, inner[index]) + inner_bias[index].astype(F32)
        act, slope = gelu_both(pre)
        acts[index] = act.astype(BF16)
        slopes[index] = slope
        residual_two = residual_two + dot_nn(acts[index], outer[index])
    unit_two, inverse_two = normed(residual_two)
    output = (unit_two * gain_two + shift_two).astype(BF16)
    grad = cotangent.reshape(amount, model).astype(F32)
    d_two = norm_pull(grad, gain_two, unit_two, inverse_two)
    d_two_low = d_two.astype(BF16)

    grads_inner, grads_outer, grads_bias = [None] * 4, [None] * 4, [None] * 4

    def far_of(parts):
        return parts[1] + links.swap(parts[3].astype(BF16), 0, 1).astype(F32)

    def near_of(parts):
        return parts[0] + links.swap(parts[2].astype(BF16), 0, 1).astype(F32)

    for index in (3, 1, 2, 0):
        grads_outer[index] = dot_tn(acts[index], d_two_low)
    far = far_of(grads_outer).astype(BF16)
    near = near_of(grads_outer)
    grad_outer = (near + links.swap(far, 0, 2).astype(F32)).astype(BF16)

    d_mid = d_two
    for index in (0, 2, 1, 3):
        d_pre = (slopes[index] * dot_nt(d_two_low, outer[index])).astype(BF16)
        grads_bias[index] = jnp.sum(d_pre.astype(F32), axis=0)
        d_mid = d_mid + dot_nt(d_pre, inner[index])
        grads_inner[index] = dot_tn(mid_low, d_pre)

    d_one = norm_pull(d_mid, gain_one, unit_one, inverse_one)
    d_one_low = d_one.astype(BF16)
    d_context = dot_nt(d_one_low, w_output).astype(BF16)
    d_context_own = d_context.reshape(own_shape)
    d_edge = links.edge(d_context_own)
    d_core = links.swap(d_context_own, 0, 1)
    head_of = lax.broadcasted_iota(jnp.int32, (16, model), 1) // (model // head_count)
    head_sum = (head_of == lax.broadcasted_iota(jnp.int32, (16, model), 0)).astype(F32)
    delta = lax.dot_general(
        head_sum,
        d_context.astype(F32) * context.astype(F32),
        (((1,), (1,)), ((), ())),
        precision=lax.Precision.HIGHEST,
        preferred_element_type=F32,
    )
    delta = jnp.transpose(delta.reshape(16, row_count, shard_len), (1, 0, 2))
    lines = jnp.concatenate([lse, delta], axis=1)
    lines_edge = links.edge(lines)
    lines_core = links.swap(lines, 0, 1)

    pair = jnp.stack([near_of(grads_inner), far_of(grads_inner)]).astype(BF16)
    pair = links.spread(pair, links.dp_stage(1), 1)
    grad_inner = pair[0].astype(F32) + links.swap(pair[1], 0, 2).astype(F32)
    grad_inner = links.around(grad_inner.astype(BF16), links.z_stages())
    grad_inner = links.collect(grad_inner, links.dp_stage(1)).astype(F32)

    grad_outer = links.spread(grad_outer, links.dp_stage(1))
    grad_outer = links.around(grad_outer, links.z_stages())
    grad_outer = links.collect(grad_outer, links.dp_stage(1)).astype(F32)

    d_query, bias_dq = pull(
        pull_query_kernel, 1, [q, k, v, d_context_own, k_core, k_edge, v_core, v_edge], [lines], [krow, qcol]
    )
    d_query = d_query.reshape(amount, model)
    grad_w_output = dot_tn(context, d_one_low).astype(BF16)
    grad_w_query = dot_tn(flat, d_query).astype(BF16)
    first = jnp.stack([links.core_spread(grad_w_output), links.core_spread(grad_w_query)])
    first = links.around(first, [links.y_stage(), links.dp_stage(1)] + links.z_stages(), 1)
    low, high = links.core_collect(first)
    grad_w_output, grad_w_query = [jnp.concatenate([low[n], high[n]], axis=1).astype(F32) for n in range(2)]

    d_pair, bias_pair = pull(
        pull_pair_kernel,
        2,
        [q, k, v, d_context_own, q_core, q_edge, d_core, d_edge],
        [lines, lines_core, lines_edge],
        [qrow, kcol],
    )
    d_pair = d_pair.reshape(amount, 2 * model)
    last = dot_tn(flat, d_pair).astype(BF16)
    last = links.core_spread(last)
    last = links.around(last, [links.plane()] + links.wide_z_stages())
    grad_w_key, grad_w_value = [half.astype(F32) for half in links.core_collect(last)]

    grad_tokens = (
        d_one
        + dot_nt(d_query, w_query)
        + dot_nt(d_pair[:, :model], w_key)
        + dot_nt(d_pair[:, model:], w_value)
    ).astype(BF16)

    def placed(bits):
        order = [bits[0], bits[2], bits[1], bits[3]]
        stacked = jnp.stack(order)
        return jnp.stack([lax.dynamic_index_in_dim(stacked, seq_at ^ a, 0, False) for a in range(4)])

    stat_rows = jnp.sum(stats, axis=0)[0:3, :]
    stat_rows = jnp.pad(stat_rows, ((0, 0), (0, model - LANES)))
    small = [jnp.sum(bias_dq[:, 0:1, :], axis=0), jnp.sum(bias_pair[:, 0:1, model:], axis=0)]
    small += [
        jnp.sum(value, axis=0, keepdims=True)
        for value in (d_one, d_mid * unit_one, d_mid, d_two, grad * unit_two, grad)
    ]
    small = links.total(jnp.concatenate(small + [stat_rows, placed(grads_bias)], axis=0))
    cluster_log = small[8:10, :head_count] / small[10:11, 0:1]
    return (
        output.reshape(own_shape),
        grad_tokens.reshape(own_shape),
        grad_w_query,
        grad_w_key,
        grad_w_value,
        grad_w_output,
        small[0],
        small[1],
        small[2],
        small[3],
        small[4],
        grad_inner,
        lax.dynamic_index_in_dim(small[11:15], seq_at, 0, False),
        grad_outer,
        small[5],
        small[6],
        small[7],
        cluster_log,
    )


def solution(mesh):
    return jax.shard_map(
        body,
        mesh=mesh,
        in_specs=(
            P("dp", "seq", None),
            P("dp", None),
            P("dp", None),
            P("dp", None, None),
            P(),
            P(),
            P(),
            P(),
            P(),
            P(),
            P(),
            P(),
            P(),
            P(None, "seq"),
            P("seq"),
            P("seq", None),
            P(),
            P(),
            P(),
            P("dp", "seq", None),
        ),
        out_specs=(
            P("dp", "seq", None),
            P("dp", "seq", None),
            P(),
            P(),
            P(),
            P(),
            P(),
            P(),
            P(),
            P(),
            P(),
            P(None, "seq"),
            P("seq"),
            P("seq", None),
            P(),
            P(),
            P(),
            P(),
        ),
        check_vma=False,
    )
```

profile of v0, /device:TPU:0, one launch (start us, length us, event | category | flops | bytes accessed | tf_op | source)
XLA Modules:
  0.0 417.6 jit_solution(15779505039124131588)
XLA Ops:
  2.7 3.2 collective-permute-start.6
  13.3 3.0 convolution_convert_fusion.8
  23.0 4.2 %codes.1 = (f32[3,128,128]{2,1,0:T(8,128)}, f32[3,128,128]{2,1,0:T(8,128)}, f32[3,128,128]{2,1,0:T(8,128)}, f32[3,128,128]{2,1,0:T(8,128)}) custom-call(s32[4]{0:T(128)} %compare_select_fusion.2.where_ref, s32[3,12,512]{2,1,0:T(8,128)} %cl_ref.1, s32[3,512]{1,0:T(4,128)} %seg_ref.1, s32[3,512]{1,0:T(4,128)} %pad_ref.1), custom_call_target="tpu_custom_call" | custom-call | tf_op jit(solution)/shard_map/codes/pallas_call | solution.py:75
  27.2 12.0 %collective-permute-done.3 = bf16[1,768]{1,0:T(2,128)(2,1)S(1)} collective-permute-done((bf16[1,768]{1,0:T(2,128)(2,1)}, bf16[1,768]{1,0:T(2,128)(2,1)S(1)}, u32[]{:S(2)}, u32[]{:S(2)}) %collective-permute-start.3) | collective-permute-done | bytes 1568 | tf_op jit(solution)/shard_map/ppermute | solution.py:309
  42.8 2.9 convolution_convert_fusion.7
  45.7 2.5 fusion.9
  48.2 2.6 fusion.10
  50.8 2.5 convolution_convert_fusion.6
  53.3 16.2 %attend.1 = (bf16[3,128,768]{2,1,0:T(8,128)(2,1)}, f32[3,16,128]{2,1,0:T(8,128)}, f32[3,8,128]{2,1,0:T(8,128)}) custom-call(bf16[3,128,768]{2,1,0:T(8,128)(2,1)} %bitcast.169, bf16[3,128,768]{2,1,0:T(8,128)(2,1)} %bitcast.166, bf16[3,128,768]{2,1,0:T(8,128)(2,1)} %bitcast.172, bf16[3,128,768]{2,1,0:T(8,128)(2,1)} %bitcast.175, ...), custom_call_target="tpu_custom_call" | custom-call | tf_op jit(solution)/shard_map/attend/pallas_call | solution.py:165
  69.5 2.2 fusion.81
  75.9 2.5 fusion.12
  78.4 2.5 fusion.13
  83.5 2.1 fusion.83
  87.6 2.4 fusion.4
  97.2 2.7 convert_reduce_fusion.3
  101.4 2.9 convert_reduce_fusion.2
  104.3 2.1 fusion.84
  117.2 10.2 %shard_map.331 = (bf16[3,128,768]{2,1,0:T(8,128)(2,1)}, f32[3,8,768]{2,1,0:T(8,128)}) custom-call(bf16[3,128,768]{2,1,0:T(8,128)(2,1)} %bitcast.170, bf16[3,128,768]{2,1,0:T(8,128)(2,1)} %bitcast.167, bf16[3,128,768]{2,1,0:T(8,128)(2,1)} %bitcast.173, bf16[3,128,768]{2,1,0:T(8,128)(2,1)} %bitcast.164, bf16[3,128,768]{2,1,0:T(8,128)(2,1)} %bitcast.176, ...), custom_call_target="tpu_custom_call" | custom-call | tf_op jit(solution)/shard_map/pallas_call | solution.py:263
  127.4 3.0 convolution_convert_fusion.3
  134.2 2.2 fusion.85
  148.5 2.6 collective-permute-start.44
  151.7 11.8 %shard_map.332 = (bf16[3,128,1536]{2,1,0:T(8,128)(2,1)}, f32[3,8,1536]{2,1,0:T(8,128)}) custom-call(bf16[3,128,768]{2,1,0:T(8,128)(2,1)} %bitcast.171, bf16[3,128,768]{2,1,0:T(8,128)(2,1)} %bitcast.168, bf16[3,128,768]{2,1,0:T(8,128)(2,1)} %bitcast.174, bf16[3,128,768]{2,1,0:T(8,128)(2,1)} %bitcast.165, bf16[3,128,768]{2,1,0:T(8,128)(2,1)} %bitcast.189, ...), custom_call_target="tpu_custom_call" | custom-call | tf_op jit(solution)/shard_map/pallas_call | solution.py:263
  171.0 13.1 %collective-permute-done.40 = f32[15,768]{1,0:T(8,128)S(1)} collective-permute-done((f32[15,768]{1,0:T(8,128)S(1)}, f32[15,768]{1,0:T(8,128)S(1)}, u32[]{:S(2)}, u32[]{:S(2)}) %collective-permute-start.40) | collective-permute-done | bytes 46112 | tf_op jit(solution)/shard_map/ppermute | solution.py:309
  192.5 3.3 collective-permute-start.43
  202.8 5.9 %collective-permute-done.17 = bf16[2,192,384]{2,1,0:T(8,128)(2,1)S(1)} collective-permute-done((bf16[2,192,384]{2,1,0:T(8,128)(2,1)S(1)}, bf16[2,192,384]{2,1,0:T(8,128)(2,1)S(1)}, u32[]{:S(2)}, u32[]{:S(2)}) %collective-permute-start.17) | collective-permute-done | bytes 294944 | tf_op jit(solution)/shard_map/ppermute | solution.py:309
  214.4 3.2 collective-permute-start.19
  220.0 3.0 collective-permute-start.20
  225.3 2.2 collective-permute-start.21
  232.4 25.8 %collective-permute-done.26 = bf16[192,768]{1,0:T(8,128)(2,1)S(1)} collective-permute-done((bf16[192,768]{1,0:T(8,128)(2,1)S(1)}, bf16[192,768]{1,0:T(8,128)(2,1)S(1)}, u32[]{:S(2)}, u32[]{:S(2)}) %collective-permute-start.26) | collective-permute-done | bytes 294944 | tf_op jit(solution)/shard_map/ppermute | solution.py:309
  259.8 4.5 %collective-permute-done.28 = bf16[192,768]{1,0:T(8,128)(2,1)S(1)} collective-permute-done((bf16[192,768]{1,0:T(8,128)(2,1)S(1)}, bf16[192,768]{1,0:T(8,128)(2,1)S(1)}, u32[]{:S(2)}, u32[]{:S(2)}) %collective-permute-start.28) | collective-permute-done | bytes 294944 | tf_op jit(solution)/shard_map/ppermute | solution.py:309
  264.4 2.2 collective-permute-start.29
  267.0 2.1 collective-permute-start.31
  276.1 3.9 collective-permute-done.32
  280.0 2.8 collective-permute-start.34
  289.2 18.2 %collective-permute-done.55 = bf16[768,768]{1,0:T(8,128)(2,1)S(1)} collective-permute-done((bf16[768,768]{1,0:T(8,128)(2,1)S(1)}, bf16[768,768]{1,0:T(8,128)(2,1)S(1)}, u32[]{:S(2)}, u32[]{:S(2)}) %collective-permute-start.55) | collective-permute-done | bytes 1179680 | tf_op jit(solution)/shard_map/ppermute | solution.py:309
  310.9 15.4 %collective-permute-done.36 = bf16[192,768]{1,0:T(8,128)(2,1)S(1)} collective-permute-done((bf16[192,768]{1,0:T(8,128)(2,1)S(1)}, bf16[192,768]{1,0:T(8,128)(2,1)S(1)}, u32[]{:S(2)}, u32[]{:S(2)}) %collective-permute-start.36) | collective-permute-done | bytes 294944 | tf_op jit(solution)/shard_map/ppermute | solution.py:309
  327.9 9.7 %collective-permute-done.47 = bf16[384,768]{1,0:T(8,128)(2,1)S(1)} collective-permute-done((bf16[384,768]{1,0:T(8,128)(2,1)S(1)}, bf16[384,768]{1,0:T(8,128)(2,1)S(1)}, u32[]{:S(2)}, u32[]{:S(2)}) %collective-permute-start.47) | collective-permute-done | bytes 589856 | tf_op jit(solution)/shard_map/ppermute | solution.py:309
  340.2 9.2 %collective-permute-done.48 = bf16[192,768]{1,0:T(8,128)(2,1)S(1)} collective-permute-done((bf16[192,768]{1,0:T(8,128)(2,1)S(1)}, bf16[192,768]{1,0:T(8,128)(2,1)S(1)}, u32[]{:S(2)}, u32[]{:S(2)}) %collective-permute-start.48) | collective-permute-done | bytes 294944 | tf_op jit(solution)/shard_map/ppermute | solution.py:309
  349.5 4.0 collective-permute-done.57
  356.0 9.0 %collective-permute-done.49 = bf16[96,768]{1,0:T(8,128)(2,1)S(1)} collective-permute-done((bf16[96,768]{1,0:T(8,128)(2,1)S(1)}, bf16[96,768]{1,0:T(8,128)(2,1)S(1)}, u32[]{:S(2)}, u32[]{:S(2)}) %collective-permute-start.49) | collective-permute-done | bytes 147488 | tf_op jit(solution)/shard_map/ppermute | solution.py:309
  365.2 6.2 %collective-permute-done.58 = bf16[96,768]{1,0:T(8,128)(2,1)S(1)} collective-permute-done((bf16[96,768]{1,0:T(8,128)(2,1)S(1)}, bf16[96,768]{1,0:T(8,128)(2,1)S(1)}, u32[]{:S(2)}, u32[]{:S(2)}) %collective-permute-start.58) | collective-permute-done | bytes 147488 | tf_op jit(solution)/shard_map/ppermute | solution.py:309
  371.5 3.0 collective-permute-done.50
  374.7 3.0 collective-permute-done.59
  377.8 2.6 select_convert_fusion
  380.3 4.2 %collective-permute-done.51 = bf16[192,768]{1,0:T(8,128)(2,1)S(1)} collective-permute-done((bf16[192,768]{1,0:T(8,128)(2,1)S(1)}, bf16[192,768]{1,0:T(8,128)(2,1)S(1)}, u32[]{:S(2)}, u32[]{:S(2)}) %collective-permute-start.51) | collective-permute-done | bytes 294944 | tf_op jit(solution)/shard_map/ppermute | solution.py:309
  384.5 4.4 %collective-permute-done.60 = bf16[192,768]{1,0:T(8,128)(2,1)S(1)} collective-permute-done((bf16[192,768]{1,0:T(8,128)(2,1)S(1)}, bf16[192,768]{1,0:T(8,128)(2,1)S(1)}, u32[]{:S(2)}, u32[]{:S(2)}) %collective-permute-start.60) | collective-permute-done | bytes 294944 | tf_op jit(solution)/shard_map/ppermute | solution.py:309
  395.2 10.2 %collective-permute-done.61 = bf16[384,768]{1,0:T(8,128)(2,1)S(1)} collective-permute-done((bf16[384,768]{1,0:T(8,128)(2,1)S(1)}, bf16[384,768]{1,0:T(8,128)(2,1)S(1)}, u32[]{:S(2)}, u32[]{:S(2)}) %collective-permute-start.61) | collective-permute-done | bytes 589856 | tf_op jit(solution)/shard_map/ppermute | solution.py:309
  407.2 8.0 %collective-permute-done.52 = bf16[384,768]{1,0:T(8,128)(2,1)S(1)} collective-permute-done((bf16[384,768]{1,0:T(8,128)(2,1)S(1)}, bf16[384,768]{1,0:T(8,128)(2,1)S(1)}, u32[]{:S(2)}, u32[]{:S(2)}) %collective-permute-start.52) | collective-permute-done | bytes 589856 | tf_op jit(solution)/shard_map/ppermute | solution.py:309
  (408 shorter events, 137.4 us)
Async XLA Ops:
  0.7 42.1 %collective-permute-start = (bf16[3,128,768]{2,1,0:T(8,128)(2,1)}, bf16[3,128,768]{2,1,0:T(8,128)(2,1)}, u32[]{:S(2)}, u32[]{:S(2)}) collective-permute-start(bf16[3,128,768]{2,1,0:T(8,128)(2,1)} %param.20), channel_id=1, source_target_pairs={{0,1},{1,0},{2,3},{3,2},{4,5},{5,4},{6,7},{7,6},{8,9},{9,8},{10,11... | collective-permute-start | bytes 1769480 | tf_op jit(solution)/shard_map/ppermute | solution.py:309
  1.2 47.0 %collective-permute-start.1 = (bf16[3,128,768]{2,1,0:T(8,128)(2,1)}, bf16[3,128,768]{2,1,0:T(8,128)(2,1)}, u32[]{:S(2)}, u32[]{:S(2)}) collective-permute-start(bf16[3,128,768]{2,1,0:T(8,128)(2,1)} %param.20), channel_id=1, source_target_pairs={{1,2},{2,1},{5,6},{6,5},{9,10},{10,9},{13,14},{14,13},{17,18},{18,... | collective-permute-start | bytes 1769480 | tf_op jit(solution)/shard_map/ppermute | solution.py:317
  2.7 78.2 %collective-permute-start.6 = (bf16[768,768]{1,0:T(8,128)(2,1)}, bf16[768,768]{1,0:T(8,128)(2,1)}, u32[]{:S(2)}, u32[]{:S(2)}) collective-permute-start(bf16[768,768]{1,0:T(8,128)(2,1)} %param.33), channel_id=1, source_target_pairs={{0,2},{1,3},{2,0},{3,1},{4,6},{5,7},{6,4},{7,5},{8,10},{9,11},{10,... | collective-permute-start | bytes 3538952 | tf_op jit(solution)/shard_map/ppermute | solution.py:309
  5.9 79.7 %collective-permute-start.2 = (bf16[768,768]{1,0:T(8,128)(2,1)}, bf16[768,768]{1,0:T(8,128)(2,1)}, u32[]{:S(2)}, u32[]{:S(2)}) collective-permute-start(bf16[768,768]{1,0:T(8,128)(2,1)} %param.33), channel_id=1, source_target_pairs={{0,1},{1,0},{2,3},{3,2},{4,5},{5,4},{6,7},{7,6},{8,9},{9,8},{10,11... | collective-permute-start | bytes 3538952 | tf_op jit(solution)/shard_map/ppermute | solution.py:309
  7.3 31.9 %collective-permute-start.3 = (bf16[1,768]{1,0:T(2,128)(2,1)}, bf16[1,768]{1,0:T(2,128)(2,1)S(1)}, u32[]{:S(2)}, u32[]{:S(2)}) collective-permute-start(bf16[1,768]{1,0:T(2,128)(2,1)} %broadcast_in_dim.48), channel_id=1, source_target_pairs={{0,2},{1,3},{2,0},{3,1},{4,6},{5,7},{6,4},{7,5},{8,10},{9,11},{10,... | collective-permute-start | bytes 4616 | tf_op jit(solution)/shard_map/ppermute | solution.py:309
  41.2 40.2 %collective-permute-start.7 = (bf16[768,768]{1,0:T(8,128)(2,1)}, bf16[768,768]{1,0:T(8,128)(2,1)}, u32[]{:S(2)}, u32[]{:S(2)}) collective-permute-start(bf16[768,768]{1,0:T(8,128)(2,1)} %param.35), channel_id=1, source_target_pairs={{0,2},{1,3},{2,0},{3,1},{4,6},{5,7},{6,4},{7,5},{8,10},{9,11},{10,... | collective-permute-start | bytes 3538952 | tf_op jit(solution)/shard_map/ppermute | solution.py:309
  42.7 44.8 %collective-permute-start.5 = (bf16[768,768]{1,0:T(8,128)(2,1)}, bf16[768,768]{1,0:T(8,128)(2,1)}, u32[]{:S(2)}, u32[]{:S(2)}) collective-permute-start(bf16[768,768]{1,0:T(8,128)(2,1)} %param.35), channel_id=1, source_target_pairs={{0,1},{1,0},{2,3},{3,2},{4,5},{5,4},{6,7},{7,6},{8,9},{9,8},{10,11... | collective-permute-start | bytes 3538952 | tf_op jit(solution)/shard_map/ppermute | solution.py:309
  80.9 9.1 %collective-permute-start.8 = (bf16[768,768]{1,0:T(8,128)(2,1)}, bf16[768,768]{1,0:T(8,128)(2,1)S(1)}, u32[]{:S(2)}, u32[]{:S(2)}) collective-permute-start(bf16[768,768]{1,0:T(8,128)(2,1)} %collective-permute-done.6), channel_id=1, source_target_pairs={{0,1},{1,0},{2,3},{3,2},{4,5},{5,4},{6,7},{7,6},{8,9},{9,8},{10,11... | collective-permute-start | bytes 3538952 | tf_op jit(solution)/shard_map/ppermute | solution.py:309
  81.4 9.4 %collective-permute-start.9 = (bf16[768,768]{1,0:T(8,128)(2,1)}, bf16[768,768]{1,0:T(8,128)(2,1)S(1)}, u32[]{:S(2)}, u32[]{:S(2)}) collective-permute-start(bf16[768,768]{1,0:T(8,128)(2,1)} %collective-permute-done.7), channel_id=1, source_target_pairs={{0,1},{1,0},{2,3},{3,2},{4,5},{5,4},{6,7},{7,6},{8,9},{9,8},{10,11... | collective-permute-start | bytes 3538952 | tf_op jit(solution)/shard_map/ppermute | solution.py:309
  112.1 39.0 %collective-permute-start.10 = (bf16[3,128,768]{2,1,0:T(8,128)(2,1)S(1)}, bf16[3,128,768]{2,1,0:T(8,128)(2,1)}, u32[]{:S(2)}, u32[]{:S(2)}) collective-permute-start(bf16[3,128,768]{2,1,0:T(8,128)(2,1)S(1)} %bitcast.162), channel_id=1, source_target_pairs={{0,1},{1,0},{2,3},{3,2},{4,5},{5,4},{6,7},{7,6},{8,9},{9,8},{10,11... | collective-permute-start | bytes 1769480 | tf_op jit(solution)/shard_map/ppermute | solution.py:309
  112.6 38.5 %collective-permute-start.11 = (bf16[3,128,768]{2,1,0:T(8,128)(2,1)S(1)}, bf16[3,128,768]{2,1,0:T(8,128)(2,1)}, u32[]{:S(2)}, u32[]{:S(2)}) collective-permute-start(bf16[3,128,768]{2,1,0:T(8,128)(2,1)S(1)} %bitcast.163), channel_id=1, source_target_pairs={{1,2},{2,1},{5,6},{6,5},{9,10},{10,9},{13,14},{14,13},{17,18},{18,... | collective-permute-start | bytes 1769480 | tf_op jit(solution)/shard_map/ppermute | solution.py:317
  115.5 29.9 %collective-permute-start.12 = (f32[3,32,128]{2,1,0:T(8,128)}, f32[3,32,128]{2,1,0:T(8,128)}, u32[]{:S(2)}, u32[]{:S(2)}) collective-permute-start(f32[3,32,128]{2,1,0:T(8,128)} %pad_maximum_fusion.10.refs_8_), channel_id=1, source_target_pairs={{0,1},{1,0},{2,3},{3,2},{4,5},{5,4},{6,7},{7,6},{8,9},{9,8},{10,11... | collective-permute-start | bytes 147464 | tf_op jit(solution)/shard_map/ppermute | solution.py:309
  139.5 25.2 %collective-permute-start.15 = (bf16[768,384]{1,0:T(8,128)(2,1)}, bf16[768,384]{1,0:T(8,128)(2,1)}, u32[]{:S(2)}, u32[]{:S(2)}) collective-permute-start(bf16[768,384]{1,0:T(8,128)(2,1)} %dynamic-slice_bitcast_fusion.1), channel_id=1, source_target_pairs={{0,1},{1,0},{2,3},{3,2},{4,5},{5,4},{6,7},{7,6},{8,9},{9,8},{10,11... | collective-permute-start | bytes 1769480 | tf_op jit(solution)/shard_map/ppermute | solution.py:309
  140.4 25.6 %collective-permute-start.14 = (bf16[768,384]{1,0:T(8,128)(2,1)}, bf16[768,384]{1,0:T(8,128)(2,1)}, u32[]{:S(2)}, u32[]{:S(2)}) collective-permute-start(bf16[768,384]{1,0:T(8,128)(2,1)} %constant_dynamic-slice_fusion.19), channel_id=1, source_target_pairs={{0,1},{1,0},{2,3},{3,2},{4,5},{5,4},{6,7},{7,6},{8,9},{9,8},{10,11... | collective-permute-start | bytes 1769480 | tf_op jit(solution)/shard_map/ppermute | solution.py:309
  148.5 62.2 %collective-permute-start.44 = (bf16[768,768]{1,0:T(8,128)(2,1)}, bf16[768,768]{1,0:T(8,128)(2,1)}, u32[]{:S(2)}, u32[]{:S(2)}) collective-permute-start(bf16[768,768]{1,0:T(8,128)(2,1)} %convolution_convert_fusion.3), channel_id=1, source_target_pairs={{0,1},{1,0},{2,3},{3,2},{4,5},{5,4},{6,7},{7,6},{8,9},{9,8},{10,11... | collective-permute-start | bytes 3538952 | tf_op jit(solution)/shard_map/ppermute | solution.py:309
  151.1 66.5 %collective-permute-start.45 = (bf16[768,768]{1,0:T(8,128)(2,1)}, bf16[768,768]{1,0:T(8,128)(2,1)}, u32[]{:S(2)}, u32[]{:S(2)}) collective-permute-start(bf16[768,768]{1,0:T(8,128)(2,1)} %convolution_convert_fusion.2), channel_id=1, source_target_pairs={{0,1},{1,0},{2,3},{3,2},{4,5},{5,4},{6,7},{7,6},{8,9},{9,8},{10,11... | collective-permute-start | bytes 3538952 | tf_op jit(solution)/shard_map/ppermute | solution.py:309
  151.1 115.9 %collective-permute-start.54 = (bf16[768,768]{1,0:T(8,128)(2,1)}, bf16[768,768]{1,0:T(8,128)(2,1)}, u32[]{:S(2)}, u32[]{:S(2)}) collective-permute-start(bf16[768,768]{1,0:T(8,128)(2,1)} %convolution_convert_fusion), channel_id=1, source_target_pairs={{0,1},{1,0},{2,3},{3,2},{4,5},{5,4},{6,7},{7,6},{8,9},{9,8},{10,11... | collective-permute-start | bytes 3538952 | tf_op jit(solution)/shard_map/ppermute | solution.py:309
  167.4 31.6 %collective-permute-start.16 = (bf16[2,384,384]{2,1,0:T(8,128)(2,1)S(1)}, bf16[2,384,384]{2,1,0:T(8,128)(2,1)S(1)}, u32[]{:S(2)}, u32[]{:S(2)}) collective-permute-start(bf16[2,384,384]{2,1,0:T(8,128)(2,1)S(1)} %fusion.60), channel_id=1, source_target_pairs={{0,2},{1,3},{2,0},{3,1},{4,6},{5,7},{6,4},{7,5},{8,10},{9,11},{10,... | collective-permute-start | bytes 1769480 | tf_op jit(solution)/shard_map/ppermute | solution.py:309
  168.4 15.8 %collective-permute-start.40 = (f32[15,768]{1,0:T(8,128)S(1)}, f32[15,768]{1,0:T(8,128)S(1)}, u32[]{:S(2)}, u32[]{:S(2)}) collective-permute-start(f32[15,768]{1,0:T(8,128)S(1)} %add.590), channel_id=1, source_target_pairs={{0,2},{1,3},{2,0},{3,1},{4,6},{5,7},{6,4},{7,5},{8,10},{9,11},{10,... | collective-permute-start | bytes 138248 | tf_op jit(solution)/shard_map/ppermute | solution.py:309
  197.8 29.7 %collective-permute-start.25 = (bf16[768,768]{1,0:T(8,128)(2,1)S(1)}, bf16[768,768]{1,0:T(8,128)(2,1)S(1)}, u32[]{:S(2)}, u32[]{:S(2)}) collective-permute-start(bf16[768,768]{1,0:T(8,128)(2,1)S(1)} %dynamic-slice_bitcast_fusion), channel_id=1, source_target_pairs={{0,1},{1,0},{2,3},{3,2},{4,5},{5,4},{6,7},{7,6},{8,9},{9,8},{10,11... | collective-permute-start | bytes 3538952 | tf_op jit(solution)/shard_map/ppermute | solution.py:309
  199.2 9.5 %collective-permute-start.17 = (bf16[2,192,384]{2,1,0:T(8,128)(2,1)S(1)}, bf16[2,192,384]{2,1,0:T(8,128)(2,1)S(1)}, u32[]{:S(2)}, u32[]{:S(2)}) collective-permute-start(bf16[2,192,384]{2,1,0:T(8,128)(2,1)S(1)} %constant_dynamic-slice_fusion.18), channel_id=1, source_target_pairs={{0,4},{1,5},{2,6},{3,7},{4,0},{5,1},{6,2},{7,3},{8,12},{9,13},{10,... | collective-permute-start | bytes 884744 | tf_op jit(solution)/shard_map/ppermute | solution.py:309
  223.0 63.7 %collective-permute-start.46 = (bf16[2,384,768]{2,1,0:T(8,128)(2,1)S(1)}, bf16[2,384,768]{2,1,0:T(8,128)(2,1)S(1)}, u32[]{:S(2)}, u32[]{:S(2)}) collective-permute-start(bf16[2,384,768]{2,1,0:T(8,128)(2,1)S(1)} %fusion.39), channel_id=1, source_target_pairs={{0,4},{1,5},{2,6},{3,7},{4,0},{5,1},{6,2},{7,3},{8,12},{9,13},{10,... | collective-permute-start | bytes 3538952 | tf_op jit(solution)/shard_map/ppermute | solution.py:309
  228.0 30.3 %collective-permute-start.26 = (bf16[192,768]{1,0:T(8,128)(2,1)S(1)}, bf16[192,768]{1,0:T(8,128)(2,1)S(1)}, u32[]{:S(2)}, u32[]{:S(2)}) collective-permute-start(bf16[192,768]{1,0:T(8,128)(2,1)S(1)} %get-tuple-element.92), channel_id=1, source_target_pairs={{0,4},{1,5},{2,6},{3,7},{4,0},{5,1},{6,2},{7,3},{8,12},{9,13},{10,... | collective-permute-start | bytes 884744 | tf_op jit(solution)/shard_map/ppermute | solution.py:309
  229.5 30.2 %collective-permute-start.27 = (bf16[192,768]{1,0:T(8,128)(2,1)S(1)}, bf16[192,768]{1,0:T(8,128)(2,1)S(1)}, u32[]{:S(2)}, u32[]{:S(2)}) collective-permute-start(bf16[192,768]{1,0:T(8,128)(2,1)S(1)} %get-tuple-element.94), channel_id=1, source_target_pairs={{0,2},{1,3},{2,0},{3,1},{4,6},{5,7},{6,4},{7,5},{8,10},{9,11},{10,... | collective-permute-start | bytes 884744 | tf_op jit(solution)/shard_map/ppermute | solution.py:309
  230.7 33.5 %collective-permute-start.28 = (bf16[192,768]{1,0:T(8,128)(2,1)S(1)}, bf16[192,768]{1,0:T(8,128)(2,1)S(1)}, u32[]{:S(2)}, u32[]{:S(2)}) collective-permute-start(bf16[192,768]{1,0:T(8,128)(2,1)S(1)} %get-tuple-element.93), channel_id=1, source_target_pairs={{0,6},{1,7},{2,4},{3,5},{4,2},{5,3},{6,0},{7,1},{8,14},{9,15},{10,... | collective-permute-start | bytes 884744 | tf_op jit(solution)/shard_map/ppermute | solution.py:309
  258.3 17.2 %collective-permute-start.22 = (bf16[2,192,384]{2,1,0:T(8,128)(2,1)S(1)}, bf16[2,192,384]{2,1,0:T(8,128)(2,1)S(1)}, u32[]{:S(2)}, u32[]{:S(2)}) collective-permute-start(bf16[2,192,384]{2,1,0:T(8,128)(2,1)S(1)} %pad_maximum_fusion.5), channel_id=1, source_target_pairs={{0,4},{1,5},{2,6},{3,7},{4,0},{5,1},{6,2},{7,3},{8,12},{9,13},{10,... | collective-permute-start | bytes 884744 | tf_op jit(solution)/shard_map/ppermute | solution.py:309
  264.4 6.8 %collective-permute-start.29 = (bf16[48,768]{1,0:T(8,128)(2,1)S(1)}, bf16[48,768]{1,0:T(8,128)(2,1)S(1)}, u32[]{:S(2)}, u32[]{:S(2)}) collective-permute-start(bf16[48,768]{1,0:T(8,128)(2,1)S(1)} %get-tuple-element.111), channel_id=1, source_target_pairs={{0,8},{1,9},{2,10},{3,11},{4,12},{5,13},{6,14},{7,15},{8,0},{9,1},... | collective-permute-start | bytes 221192 | tf_op jit(solution)/shard_map/ppermute | solution.py:309
  267.0 6.7 %collective-permute-start.31 = (bf16[48,768]{1,0:T(8,128)(2,1)S(1)}, bf16[48,768]{1,0:T(8,128)(2,1)S(1)}, u32[]{:S(2)}, u32[]{:S(2)}) collective-permute-start(bf16[48,768]{1,0:T(8,128)(2,1)S(1)} %get-tuple-element.112), channel_id=1, source_target_pairs={{0,24},{1,25},{2,26},{3,27},{4,28},{5,29},{6,30},{7,31},{8,16},{9,... | collective-permute-start | bytes 221192 | tf_op jit(solution)/shard_map/ppermute | solution.py:309
  271.2 17.3 %collective-permute-start.53 = (bf16[768,768]{1,0:T(8,128)(2,1)S(1)}, bf16[768,768]{1,0:T(8,128)(2,1)S(1)}, u32[]{:S(2)}, u32[]{:S(2)}) collective-permute-start(bf16[768,768]{1,0:T(8,128)(2,1)S(1)} %copy-done.82), channel_id=1, source_target_pairs={{0,1},{1,0},{2,3},{3,2},{4,5},{5,4},{6,7},{7,6},{8,9},{9,8},{10,11... | collective-permute-start | bytes 3538952 | tf_op jit(solution)/shard_map/ppermute | solution.py:309
  272.2 35.2 %collective-permute-start.55 = (bf16[768,768]{1,0:T(8,128)(2,1)S(1)}, bf16[768,768]{1,0:T(8,128)(2,1)S(1)}, u32[]{:S(2)}, u32[]{:S(2)}) collective-permute-start(bf16[768,768]{1,0:T(8,128)(2,1)S(1)} %add_convert_fusion.1), channel_id=1, source_target_pairs={{0,2},{1,3},{2,0},{3,1},{4,6},{5,7},{6,4},{7,5},{8,10},{9,11},{10,... | collective-permute-start | bytes 3538952 | tf_op jit(solution)/shard_map/ppermute | solution.py:309
  275.5 7.6 %collective-permute-start.33 = (bf16[48,768]{1,0:T(8,128)(2,1)S(1)}, bf16[48,768]{1,0:T(8,128)(2,1)S(1)}, u32[]{:S(2)}, u32[]{:S(2)}) collective-permute-start(bf16[48,768]{1,0:T(8,128)(2,1)S(1)} %add_convert_fusion.16), channel_id=1, source_target_pairs={{0,16},{1,17},{2,18},{3,19},{4,20},{5,21},{6,22},{7,23},{8,24},{9,... | collective-permute-start | bytes 221192 | tf_op jit(solution)/shard_map/ppermute | solution.py:309
  283.1 43.9 %collective-permute-start.23 = (bf16[2,384,384]{2,1,0:T(8,128)(2,1)S(1)}, bf16[2,384,384]{2,1,0:T(8,128)(2,1)S(1)}, u32[]{:S(2)}, u32[]{:S(2)}) collective-permute-start(bf16[2,384,384]{2,1,0:T(8,128)(2,1)S(1)} %pad_maximum_fusion.2), channel_id=1, source_target_pairs={{0,2},{1,3},{2,0},{3,1},{4,6},{5,7},{6,4},{7,5},{8,10},{9,11},{10,... | collective-permute-start | bytes 1769480 | tf_op jit(solution)/shard_map/ppermute | solution.py:309
  285.1 24.2 %collective-permute-start.35 = (bf16[192,768]{1,0:T(8,128)(2,1)S(1)}, bf16[192,768]{1,0:T(8,128)(2,1)S(1)}, u32[]{:S(2)}, u32[]{:S(2)}) collective-permute-start(bf16[192,768]{1,0:T(8,128)(2,1)S(1)} %pad_maximum_fusion.6), channel_id=1, source_target_pairs={{0,6},{1,7},{2,4},{3,5},{4,2},{5,3},{6,0},{7,1},{8,14},{9,15},{10,... | collective-permute-start | bytes 884744 | tf_op jit(solution)/shard_map/ppermute | solution.py:309
  286.8 39.6 %collective-permute-start.36 = (bf16[192,768]{1,0:T(8,128)(2,1)S(1)}, bf16[192,768]{1,0:T(8,128)(2,1)S(1)}, u32[]{:S(2)}, u32[]{:S(2)}) collective-permute-start(bf16[192,768]{1,0:T(8,128)(2,1)S(1)} %pad_maximum_fusion.6), channel_id=1, source_target_pairs={{0,2},{1,3},{2,0},{3,1},{4,6},{5,7},{6,4},{7,5},{8,10},{9,11},{10,... | collective-permute-start | bytes 884744 | tf_op jit(solution)/shard_map/ppermute | solution.py:309
  288.5 37.8 %collective-permute-start.37 = (bf16[192,768]{1,0:T(8,128)(2,1)S(1)}, bf16[192,768]{1,0:T(8,128)(2,1)S(1)}, u32[]{:S(2)}, u32[]{:S(2)}) collective-permute-start(bf16[192,768]{1,0:T(8,128)(2,1)S(1)} %pad_maximum_fusion.6), channel_id=1, source_target_pairs={{0,4},{1,5},{2,6},{3,7},{4,0},{5,1},{6,2},{7,3},{8,12},{9,13},{10,... | collective-permute-start | bytes 884744 | tf_op jit(solution)/shard_map/ppermute | solution.py:309
  307.4 30.2 %collective-permute-start.47 = (bf16[384,768]{1,0:T(8,128)(2,1)S(1)}, bf16[384,768]{1,0:T(8,128)(2,1)S(1)}, u32[]{:S(2)}, u32[]{:S(2)}) collective-permute-start(bf16[384,768]{1,0:T(8,128)(2,1)S(1)} %slice_bitcast_fusion), channel_id=1, source_target_pairs={{0,2},{1,3},{2,0},{3,1},{4,6},{5,7},{6,4},{7,5},{8,10},{9,11},{10,... | collective-permute-start | bytes 1769480 | tf_op jit(solution)/shard_map/ppermute | solution.py:309
  309.4 29.6 %collective-permute-start.56 = (bf16[384,768]{1,0:T(8,128)(2,1)S(1)}, bf16[384,768]{1,0:T(8,128)(2,1)S(1)}, u32[]{:S(2)}, u32[]{:S(2)}) collective-permute-start(bf16[384,768]{1,0:T(8,128)(2,1)S(1)} %constant_dynamic-slice_fusion.2), channel_id=1, source_target_pairs={{0,4},{1,5},{2,6},{3,7},{4,0},{5,1},{6,2},{7,3},{8,12},{9,13},{10,... | collective-permute-start | bytes 1769480 | tf_op jit(solution)/shard_map/ppermute | solution.py:309
  326.9 50.9 %collective-permute-start.38 = (bf16[768,768]{1,0:T(8,128)(2,1)S(1)}, bf16[768,768]{1,0:T(8,128)(2,1)S(1)}, u32[]{:S(2)}, u32[]{:S(2)}) collective-permute-start(bf16[768,768]{1,0:T(8,128)(2,1)S(1)} %pad_maximum_fusion.1), channel_id=1, source_target_pairs={{0,1},{1,0},{2,3},{3,2},{4,5},{5,4},{6,7},{7,6},{8,9},{9,8},{10,11... | collective-permute-start | bytes 3538952 | tf_op jit(solution)/shard_map/ppermute | solution.py:309
  327.3 64.0 %collective-permute-start.24 = (bf16[2,768,384]{2,1,0:T(8,128)(2,1)S(1)}, bf16[2,768,384]{2,1,0:T(8,128)(2,1)S(1)}, u32[]{:S(2)}, u32[]{:S(2)}) collective-permute-start(bf16[2,768,384]{2,1,0:T(8,128)(2,1)S(1)} %pad_maximum_fusion), channel_id=1, source_target_pairs={{0,1},{1,0},{2,3},{3,2},{4,5},{5,4},{6,7},{7,6},{8,9},{9,8},{10,11... | collective-permute-start | bytes 3538952 | tf_op jit(solution)/shard_map/ppermute | solution.py:309
  337.8 11.5 %collective-permute-start.48 = (bf16[192,768]{1,0:T(8,128)(2,1)S(1)}, bf16[192,768]{1,0:T(8,128)(2,1)S(1)}, u32[]{:S(2)}, u32[]{:S(2)}) collective-permute-start(bf16[192,768]{1,0:T(8,128)(2,1)S(1)} %constant_dynamic-slice_fusion.5), channel_id=1, source_target_pairs={{0,8},{1,9},{2,10},{3,11},{4,12},{5,13},{6,14},{7,15},{8,0},{9,1},... | collective-permute-start | bytes 884744 | tf_op jit(solution)/shard_map/ppermute | solution.py:309
  339.1 14.4 %collective-permute-start.57 = (bf16[192,768]{1,0:T(8,128)(2,1)S(1)}, bf16[192,768]{1,0:T(8,128)(2,1)S(1)}, u32[]{:S(2)}, u32[]{:S(2)}) collective-permute-start(bf16[192,768]{1,0:T(8,128)(2,1)S(1)} %constant_dynamic-slice_fusion.1), channel_id=1, source_target_pairs={{0,8},{1,9},{2,10},{3,11},{4,12},{5,13},{6,14},{7,15},{8,0},{9,1},... | collective-permute-start | bytes 884744 | tf_op jit(solution)/shard_map/ppermute | solution.py:309
  349.4 15.6 %collective-permute-start.49 = (bf16[96,768]{1,0:T(8,128)(2,1)S(1)}, bf16[96,768]{1,0:T(8,128)(2,1)S(1)}, u32[]{:S(2)}, u32[]{:S(2)}) collective-permute-start(bf16[96,768]{1,0:T(8,128)(2,1)S(1)} %constant_dynamic-slice_fusion.4), channel_id=1, source_target_pairs={{0,16},{1,17},{2,18},{3,19},{4,20},{5,21},{6,22},{7,23},{8,24},{9,... | collective-permute-start | bytes 442376 | tf_op jit(solution)/shard_map/ppermute | solution.py:309
  353.9 17.4 %collective-permute-start.58 = (bf16[96,768]{1,0:T(8,128)(2,1)S(1)}, bf16[96,768]{1,0:T(8,128)(2,1)S(1)}, u32[]{:S(2)}, u32[]{:S(2)}) collective-permute-start(bf16[96,768]{1,0:T(8,128)(2,1)S(1)} %constant_dynamic-slice_fusion), channel_id=1, source_target_pairs={{0,16},{1,17},{2,18},{3,19},{4,20},{5,21},{6,22},{7,23},{8,24},{9,... | collective-permute-start | bytes 442376 | tf_op jit(solution)/shard_map/ppermute | solution.py:309
  365.1 9.4 %collective-permute-start.50 = (bf16[96,768]{1,0:T(8,128)(2,1)S(1)}, bf16[96,768]{1,0:T(8,128)(2,1)S(1)}, u32[]{:S(2)}, u32[]{:S(2)}) collective-permute-start(bf16[96,768]{1,0:T(8,128)(2,1)S(1)} %add_convert_fusion.14), channel_id=1, source_target_pairs={{0,16},{1,17},{2,18},{3,19},{4,20},{5,21},{6,22},{7,23},{8,24},{9,... | collective-permute-start | bytes 442376 | tf_op jit(solution)/shard_map/ppermute | solution.py:309
  374.6 9.9 %collective-permute-start.51 = (bf16[192,768]{1,0:T(8,128)(2,1)S(1)}, bf16[192,768]{1,0:T(8,128)(2,1)S(1)}, u32[]{:S(2)}, u32[]{:S(2)}) collective-permute-start(bf16[192,768]{1,0:T(8,128)(2,1)S(1)} %pad_maximum_fusion.7), channel_id=1, source_target_pairs={{0,8},{1,9},{2,10},{3,11},{4,12},{5,13},{6,14},{7,15},{8,0},{9,1},... | collective-permute-start | bytes 884744 | tf_op jit(solution)/shard_map/ppermute | solution.py:309
  377.7 11.2 %collective-permute-start.60 = (bf16[192,768]{1,0:T(8,128)(2,1)S(1)}, bf16[192,768]{1,0:T(8,128)(2,1)S(1)}, u32[]{:S(2)}, u32[]{:S(2)}) collective-permute-start(bf16[192,768]{1,0:T(8,128)(2,1)S(1)} %pad_maximum_fusion.8), channel_id=1, source_target_pairs={{0,8},{1,9},{2,10},{3,11},{4,12},{5,13},{6,14},{7,15},{8,0},{9,1},... | collective-permute-start | bytes 884744 | tf_op jit(solution)/shard_map/ppermute | solution.py:309
  389.2 16.3 %collective-permute-start.61 = (bf16[384,768]{1,0:T(8,128)(2,1)S(1)}, bf16[384,768]{1,0:T(8,128)(2,1)S(1)}, u32[]{:S(2)}, u32[]{:S(2)}) collective-permute-start(bf16[384,768]{1,0:T(8,128)(2,1)S(1)} %pad_maximum_fusion.4), channel_id=1, source_target_pairs={{0,4},{1,5},{2,6},{3,7},{4,0},{5,1},{6,2},{7,3},{8,12},{9,13},{10,... | collective-permute-start | bytes 1769480 | tf_op jit(solution)/shard_map/ppermute | solution.py:309
  390.8 24.5 %collective-permute-start.52 = (bf16[384,768]{1,0:T(8,128)(2,1)S(1)}, bf16[384,768]{1,0:T(8,128)(2,1)S(1)}, u32[]{:S(2)}, u32[]{:S(2)}) collective-permute-start(bf16[384,768]{1,0:T(8,128)(2,1)S(1)} %pad_maximum_fusion.3), channel_id=1, source_target_pairs={{0,4},{1,5},{2,6},{3,7},{4,0},{5,1},{6,2},{7,3},{8,12},{9,13},{10,... | collective-permute-start | bytes 1769480 | tf_op jit(solution)/shard_map/ppermute | solution.py:309
  (97 other events, 532.9 us)
where the time goes:
time: 425 us; the launch traced here: 418 us
  waiting for transfers between devices  180 us (42%)
  matrix products  75 us (18%)
  starting transfers between devices  70.7 us (17%)
  Pallas kernels  43.8 us (10%)
  other arithmetic  31.3 us (7%)
  local copies, waits for them, and re-layouts  13.8 us (3%)
    ppermute x59, waiting for transfers between devices, swap(): return lax.ppermute(value, AXES, pairs)  180 us
    ppermute x59, starting transfers between devices, swap(): return lax.ppermute(value, AXES, pairs)  67.1 us
    dot_general x18, matrix products, dot_nn(): lax.dot_general(left, right, (((1,), (0,)), ((), ())), preferred_element_...  34.8 us
    pallas_call x2, Pallas kernels, pull(): pl.pallas_call(lambda *refs: kernel(model, *refs), out_shape=(jax.ShapeDt...  22 us
    dot_general x11, matrix products, dot_tn(): lax.dot_general(left, right, (((0,), (0,)), ((), ())), preferred_element_...  20 us
    dot_general x12, matrix products, dot_nt(): lax.dot_general(left, right, (((1,), (1,)), ((), ())), preferred_element_...  19.4 us
    pallas_call x1, Pallas kernels, attend(): pl.pallas_call(lambda *refs: attend_kernel(model, *refs), out_shape=(jax....  16.2 us
  transfers between devices with their start and end apart: 62, of which 30 were waited for; matrix products, arithmetic and copies ran while one was open for 23% of the time, Pallas kernels for 10%

commit v1 on v0

--- a/solution.py
+++ b/solution.py
@@ -290,8 +290,133 @@
 
 def gelu_both(value):
     cdf = 0.5 * (1.0 + lax.erf(value * (0.5**0.5)))
-    density = jnp.exp(-0.5 * value * value) * 0.3989422804014327
-    return value * cdf, cdf + value * density
+    return value * cdf, cdf + value * (jnp.exp(-0.5 * value * value) * 0.3989422804014327)
+
+
+CHUNK = 16
+ORDER = (0, 2, 1, 3)
+
+
+def back_kernel(
+    low_ref,
+    d_two_ref,
+    res_ref,
+    gain_ref,
+    ctx_ref,
+    lse_ref,
+    out_hbm,
+    slope_hbm,
+    outer_hbm,
+    inner_hbm,
+    d_pre_ref,
+    d_one_ref,
+    d_one_low_ref,
+    d_ctx_ref,
+    line_ref,
+    sum_ref,
+    out_buf,
+    slope_buf,
+    outer_buf,
+    inner_buf,
+    work_ref,
+    mid_ref,
+    sems,
+):
+    amount, model = low_ref.shape
+    moves = [None] * 13
+    for index in ORDER:
+        parts = ((outer_hbm, outer_buf), (slope_hbm, slope_buf), (inner_hbm, inner_buf))
+        for kind, (source, target) in enumerate(parts):
+            at = kind * 4 + index
+            moves[at] = pltpu.make_async_copy(source[index], target.at[index], sems.at[at])
+            moves[at].start()
+    moves[12] = pltpu.make_async_copy(out_hbm, out_buf, sems.at[12])
+    moves[12].start()
+    steps = amount // CHUNK
+    zero = jnp.zeros((8, model), F32)
+
+    def folded(value):
+        return value[:8] + value[8:]
+
+    sum_ref[...] = zero
+    for turn, index in enumerate(ORDER):
+        moves[index].wait()
+        moves[4 + index].wait()
+        work_ref[...] = dot_nt(low_ref[...], outer_buf[index])
+
+        def scale(step, total, index=index):
+            rows = pl.ds(pl.multiple_of(step * CHUNK, CHUNK), CHUNK)
+            value = (slope_buf[index, rows, :] * work_ref[rows, :]).astype(BF16)
+            d_pre_ref[index, rows, :] = value
+            return total + folded(value.astype(F32))
+
+        total = lax.fori_loop(0, steps, scale, zero)
+        sum_ref[index : index + 1, :] = jnp.sum(total, axis=0, keepdims=True)
+        moves[8 + index].wait()
+        pulled = dot_nt(d_pre_ref[index], inner_buf[index])
+        mid_ref[...] = (d_two_ref[...] if turn == 0 else mid_ref[...]) + pulled
+
+    def norm(step, totals):
+        rows = pl.ds(pl.multiple_of(step * CHUNK, CHUNK), CHUNK)
+        unit, inverse = normed(res_ref[rows, :])
+        d_mid = mid_ref[rows, :]
+        d_one = norm_pull(d_mid, gain_ref[...], unit, inverse)
+        d_one_ref[rows, :] = d_one
+        d_one_low_ref[rows, :] = d_one.astype(BF16)
+        news = (d_one, d_mid * unit, d_mid)
+        return tuple(total + folded(new) for total, new in zip(totals, news))
+
+    totals = lax.fori_loop(0, steps, norm, (zero,) * 3)
+    for index, total in enumerate(totals):
+        sum_ref[4 + index : 5 + index, :] = jnp.sum(total, axis=0, keepdims=True)
+    moves[12].wait()
+    d_ctx_ref[...] = dot_nt(d_one_low_ref[...], out_buf[...]).astype(BF16)
+    heads = (16, model)
+    head_count = 2 * model // LANES
+    head_of = lax.broadcasted_iota(jnp.int32, heads, 1) // (model // head_count)
+    head_sum = (head_of == lax.broadcasted_iota(jnp.int32, heads, 0)).astype(F32)
+    for row in range(amount // LANES):
+        rows = slice(row * LANES, (row + 1) * LANES)
+        line_ref[row, 0:16, :] = lse_ref[row]
+        line_ref[row, 16:32, :] = lax.dot_general(
+            head_sum,
+            d_ctx_ref[rows, :].astype(F32) * ctx_ref[rows, :].astype(F32),
+            (((1,), (1,)), ((), ())),
+            precision=lax.Precision.HIGHEST,
+            preferred_element_type=F32,
+        )
+
+
+def back(low, d_two, residual, gain, context, lse, w_output, slopes, outer, inner):
+    amount, model = low.shape
+    here = pl.BlockSpec(memory_space=pltpu.VMEM)
+    there = pl.BlockSpec(memory_space=pl.ANY)
+    square = (4, model, model)
+    return pl.pallas_call(
+        lambda *refs: back_kernel(
+            *refs[:7], refs[7:11], refs[11:15], refs[15:19], *refs[19:]
+        ),
+        out_shape=(
+            jax.ShapeDtypeStruct((4, amount, model), BF16),
+            jax.ShapeDtypeStruct((amount, model), F32),
+            jax.ShapeDtypeStruct((amount, model), BF16),
+            jax.ShapeDtypeStruct((amount, model), BF16),
+            jax.ShapeDtypeStruct((amount // LANES, 32, LANES), F32),
+            jax.ShapeDtypeStruct((8, model), F32),
+        ),
+        in_specs=[here] * 6 + [there] * 13,
+        out_specs=(here,) * 6,
+        scratch_shapes=[
+            pltpu.VMEM((model, model), BF16),
+            pltpu.VMEM((4, amount, model), F32),
+            pltpu.VMEM(square, BF16),
+            pltpu.VMEM(square, BF16),
+            pltpu.VMEM((amount, model), F32),
+            pltpu.VMEM((amount, model), F32),
+            pltpu.SemaphoreType.DMA((13,)),
+        ],
+        name="back",
+    )(low, d_two, residual, gain, context, lse, w_output, *slopes, *outer, *inner)
 
 
 class Links:
@@ -327,15 +452,6 @@
 
     def z_stages(self):
         return [self.dp_stage(bit) for bit in self.bits]
-
-    def wide_z_stages(self):
-        stages, stride = [], 2
-        while stride < self.dp:
-            radix = min(4, self.dp // stride)
-            partners = [(j * stride, 0) for j in range(radix)]
-            stages.append((partners, (self.dp_at // stride) % radix, "w%d" % stride))
-            stride *= radix
-        return stages
 
     def spread(self, value, stage, axis=0):
         partners, mine, _ = stage
@@ -377,6 +493,12 @@
         while stride < self.dp:
             value = value + self.swap(value, stride, 0)
             stride *= 2
+        return value
+
+    def doubled(self, value):
+        for bit in self.bits:
+            other = self.swap(value, bit, 0)
+            value = (value.astype(F32) + other.astype(F32)).astype(BF16)
         return value
 
     def around(self, value, stages, axis=0):
@@ -459,17 +581,15 @@
 
     x = flat.astype(F32)
     residual_one = x + dot_nn(context, w_output) + bias_output
-    unit_one, inverse_one = normed(residual_one)
+    unit_one, _ = normed(residual_one)
     mid = unit_one * gain_one + shift_one
     mid_low = mid.astype(BF16)
 
     acts, slopes = [None] * 4, [None] * 4
     residual_two = mid + bias_outer
     for index in (0, 2, 1, 3):
-        pre = dot_nn(mid_low, inner[index]) + inner_bias[index].astype(F32)
-        act, slope = gelu_both(pre)
+        act, slopes[index] = gelu_both(dot_nn(mid_low, inner[index]) + inner_bias[index].astype(F32))
         acts[index] = act.astype(BF16)
-        slopes[index] = slope
         residual_two = residual_two + dot_nn(acts[index], outer[index])
     unit_two, inverse_two = normed(residual_two)
     output = (unit_two * gain_two + shift_two).astype(BF16)
@@ -477,7 +597,7 @@
     d_two = norm_pull(grad, gain_two, unit_two, inverse_two)
     d_two_low = d_two.astype(BF16)
 
-    grads_inner, grads_outer, grads_bias = [None] * 4, [None] * 4, [None] * 4
+    grads_inner, grads_outer = [None] * 4, [None] * 4
 
     def far_of(parts):
         return parts[1] + links.swap(parts[3].astype(BF16), 0, 1).astype(F32)
@@ -491,30 +611,14 @@
     near = near_of(grads_outer)
     grad_outer = (near + links.swap(far, 0, 2).astype(F32)).astype(BF16)
 
-    d_mid = d_two
-    for index in (0, 2, 1, 3):
-        d_pre = (slopes[index] * dot_nt(d_two_low, outer[index])).astype(BF16)
-        grads_bias[index] = jnp.sum(d_pre.astype(F32), axis=0)
-        d_mid = d_mid + dot_nt(d_pre, inner[index])
-        grads_inner[index] = dot_tn(mid_low, d_pre)
-
-    d_one = norm_pull(d_mid, gain_one, unit_one, inverse_one)
-    d_one_low = d_one.astype(BF16)
-    d_context = dot_nt(d_one_low, w_output).astype(BF16)
+    d_pre, d_one, d_one_low, d_context, lines, sums = back(
+        d_two_low, d_two, residual_one, gain_one, context, lse, w_output, slopes, outer, inner
+    )
+    for index in (3, 1, 2, 0):
+        grads_inner[index] = dot_tn(mid_low, d_pre[index])
     d_context_own = d_context.reshape(own_shape)
     d_edge = links.edge(d_context_own)
     d_core = links.swap(d_context_own, 0, 1)
-    head_of = lax.broadcasted_iota(jnp.int32, (16, model), 1) // (model // head_count)
-    head_sum = (head_of == lax.broadcasted_iota(jnp.int32, (16, model), 0)).astype(F32)
-    delta = lax.dot_general(
-        head_sum,
-        d_context.astype(F32) * context.astype(F32),
-        (((1,), (1,)), ((), ())),
-        precision=lax.Precision.HIGHEST,
-        preferred_element_type=F32,
-    )
-    delta = jnp.transpose(delta.reshape(16, row_count, shard_len), (1, 0, 2))
-    lines = jnp.concatenate([lse, delta], axis=1)
     lines_edge = links.edge(lines)
     lines_core = links.swap(lines, 0, 1)
 
@@ -535,7 +639,11 @@
     grad_w_output = dot_tn(context, d_one_low).astype(BF16)
     grad_w_query = dot_tn(flat, d_query).astype(BF16)
     first = jnp.stack([links.core_spread(grad_w_output), links.core_spread(grad_w_query)])
-    first = links.around(first, [links.y_stage(), links.dp_stage(1)] + links.z_stages(), 1)
+    for stage in (links.y_stage(), links.dp_stage(1)):
+        first = links.spread(first, stage, 1)
+    first = links.doubled(first)
+    for stage in (links.dp_stage(1), links.y_stage()):
+        first = links.collect(first, stage, 1)
     low, high = links.core_collect(first)
     grad_w_output, grad_w_query = [jnp.concatenate([low[n], high[n]], axis=1).astype(F32) for n in range(2)]
 
@@ -549,7 +657,9 @@
     d_pair = d_pair.reshape(amount, 2 * model)
     last = dot_tn(flat, d_pair).astype(BF16)
     last = links.core_spread(last)
-    last = links.around(last, [links.plane()] + links.wide_z_stages())
+    last = links.spread(last, links.plane())
+    last = links.doubled(last)
+    last = links.collect(last, links.plane())
     grad_w_key, grad_w_value = [half.astype(F32) for half in links.core_collect(last)]
 
     grad_tokens = (
@@ -559,19 +669,16 @@
         + dot_nt(d_pair[:, model:], w_value)
     ).astype(BF16)
 
-    def placed(bits):
-        order = [bits[0], bits[2], bits[1], bits[3]]
-        stacked = jnp.stack(order)
-        return jnp.stack([lax.dynamic_index_in_dim(stacked, seq_at ^ a, 0, False) for a in range(4)])
-
+    bias_rows = [sums[0:1], sums[2:3], sums[1:2], sums[3:4]]
+    for bit in (1, 2):
+        odd = (seq_at // bit) % 2 == 1
+        bias_rows = [jnp.where(odd, bias_rows[n ^ bit], bias_rows[n]) for n in range(4)]
     stat_rows = jnp.sum(stats, axis=0)[0:3, :]
     stat_rows = jnp.pad(stat_rows, ((0, 0), (0, model - LANES)))
-    small = [jnp.sum(bias_dq[:, 0:1, :], axis=0), jnp.sum(bias_pair[:, 0:1, model:], axis=0)]
-    small += [
-        jnp.sum(value, axis=0, keepdims=True)
-        for value in (d_one, d_mid * unit_one, d_mid, d_two, grad * unit_two, grad)
-    ]
-    small = links.total(jnp.concatenate(small + [stat_rows, placed(grads_bias)], axis=0))
+    small = [jnp.sum(bias_dq[:, 0:1, :], axis=0), jnp.sum(bias_pair[:, 0:1, model:], axis=0), sums[4:7]]
+    small += [jnp.sum(value, axis=0, keepdims=True) for value in (d_two, grad * unit_two, grad)]
+    small += [stat_rows] + bias_rows
+    small = links.total(jnp.concatenate(small, axis=0))
     cluster_log = small[8:10, :head_count] / small[10:11, 0:1]
     return (
         output.reshape(own_shape),

time: 425 us -> 386 us (0.908)
  waiting for transfers between devices: 180 us -> 151 us
  starting transfers between devices: 70.7 us -> 49.1 us
  Pallas kernels: 43.8 us -> 64.5 us
  matrix products: 75 us -> 63.4 us
    ppermute x59 -> x53, waiting for transfers between devices: 180 us -> 151 us  [swap(): return lax.ppermute(value, AXES, pairs)]
    ppermute x59 -> x53, starting transfers between devices: 67.1 us -> 46.3 us  [swap(): return lax.ppermute(value, AXES, pairs)]
    pallas_call x0 -> x1, Pallas kernels: none -> 20.7 us  [back(): pl.pallas_call(lambda *refs: back_kernel(*refs[:7], refs[7:11], refs[11:1...]
    dot_general x12 -> x3, matrix products: 19.4 us -> 2.98 us  [dot_nt(): lax.dot_general(left, right, (((1,), (1,)), ((), ())), preferred_element_...]
    dot_general x18, matrix products: 34.8 us -> 40.5 us  [dot_nn(): lax.dot_general(left, right, (((1,), (0,)), ((), ())), preferred_element_...]
  transfers between devices with their start and end apart: 62 -> 56, of which waited for: 30 -> 22; matrix products, arithmetic and copies ran while one was open for 23% -> 26% of each run, Pallas kernels for 10% -> 12%
where the time goes in v1:
time: 386 us; the launch traced here: 378 us
  waiting for transfers between devices  151 us (39%)
  Pallas kernels  64.5 us (17%)
  matrix products  63.4 us (16%)
  starting transfers between devices  49.1 us (13%)
  other arithmetic  31.7 us (8%)
  local copies, waits for them, and re-layouts  16.7 us (4%)
    ppermute x53, waiting for transfers between devices, swap(): return lax.ppermute(value, AXES, pairs)  151 us
    ppermute x53, starting transfers between devices, swap(): return lax.ppermute(value, AXES, pairs)  46.3 us
    dot_general x18, matrix products, dot_nn(): lax.dot_general(left, right, (((1,), (0,)), ((), ())), preferred_element_...  40.5 us
    pallas_call x2, Pallas kernels, pull(): pl.pallas_call(lambda *refs: kernel(model, *refs), out_shape=(jax.ShapeDt...  22 us
    pallas_call x1, Pallas kernels, back(): pl.pallas_call(lambda *refs: back_kernel(*refs[:7], refs[7:11], refs[11:1...  20.7 us
    dot_general x11, matrix products, dot_tn(): lax.dot_general(left, right, (((0,), (0,)), ((), ())), preferred_element_...  19.9 us
    pallas_call x1, Pallas kernels, attend(): pl.pallas_call(lambda *refs: attend_kernel(model, *refs), out_shape=(jax....  16.2 us
  transfers between devices with their start and end apart: 56, of which 22 were waited for; matrix products, arithmetic and copies ran while one was open for 26% of the time, Pallas kernels for 12%

profile of v1, /device:TPU:0, one launch (start us, length us, event | category | flops | bytes accessed | tf_op | source)
XLA Modules:
  0.0 378.5 jit_solution(9808148588011476927)
XLA Ops:
  2.7 3.2 collective-permute-start.6
  10.4 2.2 slice_reduce_fusion.11
  12.7 3.0 convolution_convert_fusion.7
  21.2 4.2 %codes.1 = (f32[3,128,128]{2,1,0:T(8,128)}, f32[3,128,128]{2,1,0:T(8,128)}, f32[3,128,128]{2,1,0:T(8,128)}, f32[3,128,128]{2,1,0:T(8,128)}) custom-call(s32[4]{0:T(128)} %compare_select_fusion.2.where_ref, s32[3,12,512]{2,1,0:T(8,128)} %cl_ref.1, s32[3,512]{1,0:T(4,128)} %seg_ref.1, s32[3,512]{1,0:T(4,128)} %pad_ref.1), custom_call_target="tpu_custom_call" | custom-call | tf_op jit(solution)/shard_map/codes/pallas_call | solution.py:75
  25.4 13.9 %collective-permute-done.3 = bf16[1,768]{1,0:T(2,128)(2,1)S(1)} collective-permute-done((bf16[1,768]{1,0:T(2,128)(2,1)}, bf16[1,768]{1,0:T(2,128)(2,1)S(1)}, u32[]{:S(2)}, u32[]{:S(2)}) %collective-permute-start.3) | collective-permute-done | bytes 1568 | tf_op jit(solution)/shard_map/ppermute | solution.py:434
  43.8 2.9 convolution_convert_fusion.6
  46.7 2.5 fusion.10
  49.2 2.6 fusion.11
  51.9 2.5 convolution_convert_fusion.5
  54.4 16.2 %attend.1 = (bf16[3,128,768]{2,1,0:T(8,128)(2,1)}, f32[3,16,128]{2,1,0:T(8,128)}, f32[3,8,128]{2,1,0:T(8,128)}) custom-call(bf16[3,128,768]{2,1,0:T(8,128)(2,1)} %bitcast.149, bf16[3,128,768]{2,1,0:T(8,128)(2,1)} %bitcast.146, bf16[3,128,768]{2,1,0:T(8,128)(2,1)} %bitcast.152, bf16[3,128,768]{2,1,0:T(8,128)(2,1)} %bitcast.155, ...), custom_call_target="tpu_custom_call" | custom-call | tf_op jit(solution)/shard_map/attend/pallas_call | solution.py:165
  70.6 2.2 fusion.63
  75.4 2.7 fusion.17
  78.9 2.6 fusion.12
  81.4 2.5 fusion.13
  84.5 3.2 fusion.21
  87.7 2.1 fusion.65
  89.9 3.1 fusion.25
  93.0 2.4 fusion.3
  102.7 20.7 %back.1 = (bf16[4,384,768]{2,1,0:T(8,128)(2,1)}, f32[384,768]{1,0:T(8,128)}, bf16[384,768]{1,0:T(8,128)(2,1)}, bf16[384,768]{1,0:T(8,128)(2,1)}, f32[3,32,128]{2,1,0:T(8,128)}, /*index=5*/f32[8,768]{1,0:T(8,128)}) custom-call(bf16[384,768]{1,0:T(8,128)(2,1)} %convert_element_type.326.refs_0_, f32[384,768]{1,0:T(8,128)} %copy-done.3, f32[384,768]{1,0:T(8,128)} %copy-done.2, ...), custom_call_target="tpu_custom_call" | custom-call | tf_op jit(solution)/shard_map/back/pallas_call | solution.py:395
  124.6 10.2 %shard_map.331 = (bf16[3,128,768]{2,1,0:T(8,128)(2,1)}, f32[3,8,768]{2,1,0:T(8,128)}) custom-call(bf16[3,128,768]{2,1,0:T(8,128)(2,1)} %bitcast.150, bf16[3,128,768]{2,1,0:T(8,128)(2,1)} %bitcast.147, bf16[3,128,768]{2,1,0:T(8,128)(2,1)} %bitcast.153, bf16[3,128,768]{2,1,0:T(8,128)(2,1)} %bitcast.165, bf16[3,128,768]{2,1,0:T(8,128)(2,1)} %bitcast.156, ...), custom_call_target="tpu_custom_call" | custom-call | tf_op jit(solution)/shard_map/pallas_call | solution.py:263
  134.8 2.2 collective-permute-start.12
  137.0 2.9 convolution_convert_fusion.3
  139.9 3.0 convolution_convert_fusion.2
  146.6 2.2 fusion.67
  158.5 2.3 collective-permute-start.38
  161.9 11.8 %shard_map.332 = (bf16[3,128,1536]{2,1,0:T(8,128)(2,1)}, f32[3,8,1536]{2,1,0:T(8,128)}) custom-call(bf16[3,128,768]{2,1,0:T(8,128)(2,1)} %bitcast.151, bf16[3,128,768]{2,1,0:T(8,128)(2,1)} %bitcast.148, bf16[3,128,768]{2,1,0:T(8,128)(2,1)} %bitcast.154, bf16[3,128,768]{2,1,0:T(8,128)(2,1)} %bitcast.166, bf16[3,128,768]{2,1,0:T(8,128)(2,1)} %bitcast.170, ...), custom_call_target="tpu_custom_call" | custom-call | tf_op jit(solution)/shard_map/pallas_call | solution.py:263
  174.6 2.7 concatenate.45
  185.6 11.3 %collective-permute-done.34 = f32[15,768]{1,0:T(8,128)S(1)} collective-permute-done((f32[15,768]{1,0:T(8,128)S(1)}, f32[15,768]{1,0:T(8,128)S(1)}, u32[]{:S(2)}, u32[]{:S(2)}) %collective-permute-start.34) | collective-permute-done | bytes 46112 | tf_op jit(solution)/shard_map/ppermute | solution.py:434
  201.1 2.1 collective-permute-start.36
  205.3 3.4 collective-permute-start.37
  220.8 3.3 collective-permute-done.18
  231.0 7.9 %collective-permute-done.19 = bf16[2,192,384]{2,1,0:T(8,128)(2,1)S(1)} collective-permute-done((bf16[2,192,384]{2,1,0:T(8,128)(2,1)S(1)}, bf16[2,192,384]{2,1,0:T(8,128)(2,1)S(1)}, u32[]{:S(2)}, u32[]{:S(2)}) %collective-permute-start.19) | collective-permute-done | bytes 294944 | tf_op jit(solution)/shard_map/ppermute | solution.py:434
  239.8 12.8 %collective-permute-done.24 = bf16[192,768]{1,0:T(8,128)(2,1)S(1)} collective-permute-done((bf16[192,768]{1,0:T(8,128)(2,1)S(1)}, bf16[192,768]{1,0:T(8,128)(2,1)S(1)}, u32[]{:S(2)}, u32[]{:S(2)}) %collective-permute-start.24) | collective-permute-done | bytes 294944 | tf_op jit(solution)/shard_map/ppermute | solution.py:434
  254.3 13.8 %collective-permute-done.25 = bf16[192,768]{1,0:T(8,128)(2,1)S(1)} collective-permute-done((bf16[192,768]{1,0:T(8,128)(2,1)S(1)}, bf16[192,768]{1,0:T(8,128)(2,1)S(1)}, u32[]{:S(2)}, u32[]{:S(2)}) %collective-permute-start.25) | collective-permute-done | bytes 294944 | tf_op jit(solution)/shard_map/ppermute | solution.py:434
  274.3 2.9 collective-permute-done.27
  278.4 11.0 %collective-permute-done.28 = bf16[192,768]{1,0:T(8,128)(2,1)S(1)} collective-permute-done((bf16[192,768]{1,0:T(8,128)(2,1)S(1)}, bf16[192,768]{1,0:T(8,128)(2,1)S(1)}, u32[]{:S(2)}, u32[]{:S(2)}) %collective-permute-start.28) | collective-permute-done | bytes 294944 | tf_op jit(solution)/shard_map/ppermute | solution.py:434
  293.5 13.0 %collective-permute-done.21 = bf16[2,384,384]{2,1,0:T(8,128)(2,1)S(1)} collective-permute-done((bf16[2,384,384]{2,1,0:T(8,128)(2,1)S(1)}, bf16[2,384,384]{2,1,0:T(8,128)(2,1)S(1)}, u32[]{:S(2)}, u32[]{:S(2)}) %collective-permute-start.21) | collective-permute-done | bytes 589856 | tf_op jit(solution)/shard_map/ppermute | solution.py:434
  307.3 2.4 collective-permute-done.30
  310.5 2.8 collective-permute-done.51
  313.7 9.7 %collective-permute-done.43 = bf16[96,768]{1,0:T(8,128)(2,1)S(1)} collective-permute-done((bf16[96,768]{1,0:T(8,128)(2,1)S(1)}, bf16[96,768]{1,0:T(8,128)(2,1)S(1)}, u32[]{:S(2)}, u32[]{:S(2)}) %collective-permute-start.43) | collective-permute-done | bytes 147488 | tf_op jit(solution)/shard_map/ppermute | solution.py:434
  323.5 9.4 %collective-permute-done.52 = bf16[96,768]{1,0:T(8,128)(2,1)S(1)} collective-permute-done((bf16[96,768]{1,0:T(8,128)(2,1)S(1)}, bf16[96,768]{1,0:T(8,128)(2,1)S(1)}, u32[]{:S(2)}, u32[]{:S(2)}) %collective-permute-start.52) | collective-permute-done | bytes 147488 | tf_op jit(solution)/shard_map/ppermute | solution.py:434
  333.0 3.0 collective-permute-done.44
  336.1 3.6 collective-permute-done.53
  339.9 6.2 %collective-permute-done.45 = bf16[192,768]{1,0:T(8,128)(2,1)S(1)} collective-permute-done((bf16[192,768]{1,0:T(8,128)(2,1)S(1)}, bf16[192,768]{1,0:T(8,128)(2,1)S(1)}, u32[]{:S(2)}, u32[]{:S(2)}) %collective-permute-start.45) | collective-permute-done | bytes 294944 | tf_op jit(solution)/shard_map/ppermute | solution.py:434
  347.1 5.2 %collective-permute-done.54 = bf16[192,768]{1,0:T(8,128)(2,1)S(1)} collective-permute-done((bf16[192,768]{1,0:T(8,128)(2,1)S(1)}, bf16[192,768]{1,0:T(8,128)(2,1)S(1)}, u32[]{:S(2)}, u32[]{:S(2)}) %collective-permute-start.54) | collective-permute-done | bytes 294944 | tf_op jit(solution)/shard_map/ppermute | solution.py:434
  357.0 2.6 select_convert_fusion
  359.5 3.2 collective-permute-done.46
  362.7 11.6 %collective-permute-done.55 = bf16[384,768]{1,0:T(8,128)(2,1)S(1)} collective-permute-done((bf16[384,768]{1,0:T(8,128)(2,1)S(1)}, bf16[384,768]{1,0:T(8,128)(2,1)S(1)}, u32[]{:S(2)}, u32[]{:S(2)}) %collective-permute-start.55) | collective-permute-done | bytes 589856 | tf_op jit(solution)/shard_map/ppermute | solution.py:434
  (322 shorter events, 103.3 us)
Async XLA Ops:
  0.7 43.1 %collective-permute-start = (bf16[3,128,768]{2,1,0:T(8,128)(2,1)}, bf16[3,128,768]{2,1,0:T(8,128)(2,1)}, u32[]{:S(2)}, u32[]{:S(2)}) collective-permute-start(bf16[3,128,768]{2,1,0:T(8,128)(2,1)} %param.20), channel_id=1, source_target_pairs={{0,1},{1,0},{2,3},{3,2},{4,5},{5,4},{6,7},{7,6},{8,9},{9,8},{10,11... | collective-permute-start | bytes 1769480 | tf_op jit(solution)/shard_map/ppermute | solution.py:434
  1.2 48.0 %collective-permute-start.1 = (bf16[3,128,768]{2,1,0:T(8,128)(2,1)}, bf16[3,128,768]{2,1,0:T(8,128)(2,1)}, u32[]{:S(2)}, u32[]{:S(2)}) collective-permute-start(bf16[3,128,768]{2,1,0:T(8,128)(2,1)} %param.20), channel_id=1, source_target_pairs={{1,2},{2,1},{5,6},{6,5},{9,10},{10,9},{13,14},{14,13},{17,18},{18,... | collective-permute-start | bytes 1769480 | tf_op jit(solution)/shard_map/ppermute | solution.py:442
  2.7 81.2 %collective-permute-start.6 = (bf16[768,768]{1,0:T(8,128)(2,1)}, bf16[768,768]{1,0:T(8,128)(2,1)}, u32[]{:S(2)}, u32[]{:S(2)}) collective-permute-start(bf16[768,768]{1,0:T(8,128)(2,1)} %refs_15_.1), channel_id=1, source_target_pairs={{0,2},{1,3},{2,0},{3,1},{4,6},{5,7},{6,4},{7,5},{8,10},{9,11},{10,... | collective-permute-start | bytes 3538952 | tf_op jit(solution)/shard_map/ppermute | solution.py:434
  5.9 84.0 %collective-permute-start.2 = (bf16[768,768]{1,0:T(8,128)(2,1)}, bf16[768,768]{1,0:T(8,128)(2,1)}, u32[]{:S(2)}, u32[]{:S(2)}) collective-permute-start(bf16[768,768]{1,0:T(8,128)(2,1)} %refs_15_.1), channel_id=1, source_target_pairs={{0,1},{1,0},{2,3},{3,2},{4,5},{5,4},{6,7},{7,6},{8,9},{9,8},{10,11... | collective-permute-start | bytes 3538952 | tf_op jit(solution)/shard_map/ppermute | solution.py:434
  7.3 31.9 %collective-permute-start.3 = (bf16[1,768]{1,0:T(2,128)(2,1)}, bf16[1,768]{1,0:T(2,128)(2,1)S(1)}, u32[]{:S(2)}, u32[]{:S(2)}) collective-permute-start(bf16[1,768]{1,0:T(2,128)(2,1)} %broadcast_in_dim.37), channel_id=1, source_target_pairs={{0,2},{1,3},{2,0},{3,1},{4,6},{5,7},{6,4},{7,5},{8,10},{9,11},{10,... | collective-permute-start | bytes 4616 | tf_op jit(solution)/shard_map/ppermute | solution.py:434
  41.9 42.5 %collective-permute-start.7 = (bf16[768,768]{1,0:T(8,128)(2,1)}, bf16[768,768]{1,0:T(8,128)(2,1)}, u32[]{:S(2)}, u32[]{:S(2)}) collective-permute-start(bf16[768,768]{1,0:T(8,128)(2,1)} %refs_11_.1), channel_id=1, source_target_pairs={{0,2},{1,3},{2,0},{3,1},{4,6},{5,7},{6,4},{7,5},{8,10},{9,11},{10,... | collective-permute-start | bytes 3538952 | tf_op jit(solution)/shard_map/ppermute | solution.py:434
  43.8 49.2 %collective-permute-start.5 = (bf16[768,768]{1,0:T(8,128)(2,1)}, bf16[768,768]{1,0:T(8,128)(2,1)}, u32[]{:S(2)}, u32[]{:S(2)}) collective-permute-start(bf16[768,768]{1,0:T(8,128)(2,1)} %refs_11_.1), channel_id=1, source_target_pairs={{0,1},{1,0},{2,3},{3,2},{4,5},{5,4},{6,7},{7,6},{8,9},{9,8},{10,11... | collective-permute-start | bytes 3538952 | tf_op jit(solution)/shard_map/ppermute | solution.py:434
  84.0 11.5 %collective-permute-start.8 = (bf16[768,768]{1,0:T(8,128)(2,1)}, bf16[768,768]{1,0:T(8,128)(2,1)S(1)}, u32[]{:S(2)}, u32[]{:S(2)}) collective-permute-start(bf16[768,768]{1,0:T(8,128)(2,1)} %collective-permute-done.6.refs_16_), channel_id=1, source_target_pairs={{0,1},{1,0},{2,3},{3,2},{4,5},{5,4},{6,7},{7,6},{8,9},{9,8},{10,11... | collective-permute-start | bytes 3538952 | tf_op jit(solution)/shard_map/ppermute | solution.py:434
  84.5 12.9 %collective-permute-start.9 = (bf16[768,768]{1,0:T(8,128)(2,1)}, bf16[768,768]{1,0:T(8,128)(2,1)S(1)}, u32[]{:S(2)}, u32[]{:S(2)}) collective-permute-start(bf16[768,768]{1,0:T(8,128)(2,1)} %collective-permute-done.7.refs_12_), channel_id=1, source_target_pairs={{0,1},{1,0},{2,3},{3,2},{4,5},{5,4},{6,7},{7,6},{8,9},{9,8},{10,11... | collective-permute-start | bytes 3538952 | tf_op jit(solution)/shard_map/ppermute | solution.py:434
  123.4 37.4 %collective-permute-start.10 = (bf16[3,128,768]{2,1,0:T(8,128)(2,1)}, bf16[3,128,768]{2,1,0:T(8,128)(2,1)S(1)}, u32[]{:S(2)}, u32[]{:S(2)}) collective-permute-start(bf16[3,128,768]{2,1,0:T(8,128)(2,1)} %bitcast.163), channel_id=1, source_target_pairs={{0,1},{1,0},{2,3},{3,2},{4,5},{5,4},{6,7},{7,6},{8,9},{9,8},{10,11... | collective-permute-start | bytes 1769480 | tf_op jit(solution)/shard_map/ppermute | solution.py:434
  123.9 37.0 %collective-permute-start.11 = (bf16[3,128,768]{2,1,0:T(8,128)(2,1)}, bf16[3,128,768]{2,1,0:T(8,128)(2,1)S(1)}, u32[]{:S(2)}, u32[]{:S(2)}) collective-permute-start(bf16[3,128,768]{2,1,0:T(8,128)(2,1)} %bitcast.164), channel_id=1, source_target_pairs={{1,2},{2,1},{5,6},{6,5},{9,10},{10,9},{13,14},{14,13},{17,18},{18,... | collective-permute-start | bytes 1769480 | tf_op jit(solution)/shard_map/ppermute | solution.py:442
  134.8 20.4 %collective-permute-start.12 = (f32[3,32,128]{2,1,0:T(8,128)}, f32[3,32,128]{2,1,0:T(8,128)S(1)}, u32[]{:S(2)}, u32[]{:S(2)}) collective-permute-start(f32[3,32,128]{2,1,0:T(8,128)} %get-tuple-element.41.refs_8_), channel_id=1, source_target_pairs={{0,1},{1,0},{2,3},{3,2},{4,5},{5,4},{6,7},{7,6},{8,9},{9,8},{10,11... | collective-permute-start | bytes 147464 | tf_op jit(solution)/shard_map/ppermute | solution.py:434
  150.6 27.0 %collective-permute-start.15 = (bf16[768,384]{1,0:T(8,128)(2,1)}, bf16[768,384]{1,0:T(8,128)(2,1)}, u32[]{:S(2)}, u32[]{:S(2)}) collective-permute-start(bf16[768,384]{1,0:T(8,128)(2,1)} %dynamic-slice_bitcast_fusion.1), channel_id=1, source_target_pairs={{0,1},{1,0},{2,3},{3,2},{4,5},{5,4},{6,7},{7,6},{8,9},{9,8},{10,11... | collective-permute-start | bytes 1769480 | tf_op jit(solution)/shard_map/ppermute | solution.py:434
  154.1 24.8 %collective-permute-start.14 = (bf16[768,384]{1,0:T(8,128)(2,1)}, bf16[768,384]{1,0:T(8,128)(2,1)}, u32[]{:S(2)}, u32[]{:S(2)}) collective-permute-start(bf16[768,384]{1,0:T(8,128)(2,1)} %constant_dynamic-slice_fusion.10), channel_id=1, source_target_pairs={{0,1},{1,0},{2,3},{3,2},{4,5},{5,4},{6,7},{7,6},{8,9},{9,8},{10,11... | collective-permute-start | bytes 1769480 | tf_op jit(solution)/shard_map/ppermute | solution.py:434
  158.5 53.9 %collective-permute-start.38 = (bf16[768,768]{1,0:T(8,128)(2,1)}, bf16[768,768]{1,0:T(8,128)(2,1)}, u32[]{:S(2)}, u32[]{:S(2)}) collective-permute-start(bf16[768,768]{1,0:T(8,128)(2,1)} %convolution_convert_fusion.3), channel_id=1, source_target_pairs={{0,1},{1,0},{2,3},{3,2},{4,5},{5,4},{6,7},{7,6},{8,9},{9,8},{10,11... | collective-permute-start | bytes 3538952 | tf_op jit(solution)/shard_map/ppermute | solution.py:434
  160.8 56.2 %collective-permute-start.39 = (bf16[768,768]{1,0:T(8,128)(2,1)}, bf16[768,768]{1,0:T(8,128)(2,1)}, u32[]{:S(2)}, u32[]{:S(2)}) collective-permute-start(bf16[768,768]{1,0:T(8,128)(2,1)} %convolution_convert_fusion.2), channel_id=1, source_target_pairs={{0,1},{1,0},{2,3},{3,2},{4,5},{5,4},{6,7},{7,6},{8,9},{9,8},{10,11... | collective-permute-start | bytes 3538952 | tf_op jit(solution)/shard_map/ppermute | solution.py:434
  180.3 28.4 %collective-permute-start.16 = (bf16[2,384,384]{2,1,0:T(8,128)(2,1)S(1)}, bf16[2,384,384]{2,1,0:T(8,128)(2,1)S(1)}, u32[]{:S(2)}, u32[]{:S(2)}) collective-permute-start(bf16[2,384,384]{2,1,0:T(8,128)(2,1)S(1)} %fusion.44), channel_id=1, source_target_pairs={{0,2},{1,3},{2,0},{3,1},{4,6},{5,7},{6,4},{7,5},{8,10},{9,11},{10,... | collective-permute-start | bytes 1769480 | tf_op jit(solution)/shard_map/ppermute | solution.py:434
  183.8 13.1 %collective-permute-start.34 = (f32[15,768]{1,0:T(8,128)S(1)}, f32[15,768]{1,0:T(8,128)S(1)}, u32[]{:S(2)}, u32[]{:S(2)}) collective-permute-start(f32[15,768]{1,0:T(8,128)S(1)} %add.506), channel_id=1, source_target_pairs={{0,2},{1,3},{2,0},{3,1},{4,6},{5,7},{6,4},{7,5},{8,10},{9,11},{10,... | collective-permute-start | bytes 138248 | tf_op jit(solution)/shard_map/ppermute | solution.py:434
  203.2 22.9 %collective-permute-start.23 = (bf16[768,768]{1,0:T(8,128)(2,1)S(1)}, bf16[768,768]{1,0:T(8,128)(2,1)S(1)}, u32[]{:S(2)}, u32[]{:S(2)}) collective-permute-start(bf16[768,768]{1,0:T(8,128)(2,1)S(1)} %dynamic-slice_bitcast_fusion), channel_id=1, source_target_pairs={{0,1},{1,0},{2,3},{3,2},{4,5},{5,4},{6,7},{7,6},{8,9},{9,8},{10,11... | collective-permute-start | bytes 3538952 | tf_op jit(solution)/shard_map/ppermute | solution.py:434
  211.9 16.2 %collective-permute-start.48 = (bf16[768,768]{1,0:T(8,128)(2,1)S(1)}, bf16[768,768]{1,0:T(8,128)(2,1)S(1)}, u32[]{:S(2)}, u32[]{:S(2)}) collective-permute-start(bf16[768,768]{1,0:T(8,128)(2,1)S(1)} %copy-done.60), channel_id=1, source_target_pairs={{0,1},{1,0},{2,3},{3,2},{4,5},{5,4},{6,7},{7,6},{8,9},{9,8},{10,11... | collective-permute-start | bytes 3538952 | tf_op jit(solution)/shard_map/ppermute | solution.py:434
  212.4 60.1 %collective-permute-start.47 = (bf16[768,768]{1,0:T(8,128)(2,1)S(1)}, bf16[768,768]{1,0:T(8,128)(2,1)S(1)}, u32[]{:S(2)}, u32[]{:S(2)}) collective-permute-start(bf16[768,768]{1,0:T(8,128)(2,1)S(1)} %copy-done.59), channel_id=1, source_target_pairs={{0,1},{1,0},{2,3},{3,2},{4,5},{5,4},{6,7},{7,6},{8,9},{9,8},{10,11... | collective-permute-start | bytes 3538952 | tf_op jit(solution)/shard_map/ppermute | solution.py:434
  215.7 8.4 %collective-permute-start.18 = (bf16[2,192,384]{2,1,0:T(8,128)(2,1)S(1)}, bf16[2,192,384]{2,1,0:T(8,128)(2,1)S(1)}, u32[]{:S(2)}, u32[]{:S(2)}) collective-permute-start(bf16[2,192,384]{2,1,0:T(8,128)(2,1)S(1)} %add_convert_fusion.17), channel_id=1, source_target_pairs={{0,8},{1,9},{2,10},{3,11},{4,12},{5,13},{6,14},{7,15},{8,0},{9,1},... | collective-permute-start | bytes 884744 | tf_op jit(solution)/shard_map/ppermute | solution.py:434
  219.3 52.0 %collective-permute-start.40 = (bf16[2,384,768]{2,1,0:T(8,128)(2,1)S(1)}, bf16[2,384,768]{2,1,0:T(8,128)(2,1)S(1)}, u32[]{:S(2)}, u32[]{:S(2)}) collective-permute-start(bf16[2,384,768]{2,1,0:T(8,128)(2,1)S(1)} %fusion.30), channel_id=1, source_target_pairs={{0,4},{1,5},{2,6},{3,7},{4,0},{5,1},{6,2},{7,3},{8,12},{9,13},{10,... | collective-permute-start | bytes 3538952 | tf_op jit(solution)/shard_map/ppermute | solution.py:434
  224.2 14.8 %collective-permute-start.19 = (bf16[2,192,384]{2,1,0:T(8,128)(2,1)S(1)}, bf16[2,192,384]{2,1,0:T(8,128)(2,1)S(1)}, u32[]{:S(2)}, u32[]{:S(2)}) collective-permute-start(bf16[2,192,384]{2,1,0:T(8,128)(2,1)S(1)} %add_convert_fusion.16), channel_id=1, source_target_pairs={{0,16},{1,17},{2,18},{3,19},{4,20},{5,21},{6,22},{7,23},{8,24},{9,... | collective-permute-start | bytes 884744 | tf_op jit(solution)/shard_map/ppermute | solution.py:434
  226.5 26.1 %collective-permute-start.24 = (bf16[192,768]{1,0:T(8,128)(2,1)S(1)}, bf16[192,768]{1,0:T(8,128)(2,1)S(1)}, u32[]{:S(2)}, u32[]{:S(2)}) collective-permute-start(bf16[192,768]{1,0:T(8,128)(2,1)S(1)} %get-tuple-element.93), channel_id=1, source_target_pairs={{0,4},{1,5},{2,6},{3,7},{4,0},{5,1},{6,2},{7,3},{8,12},{9,13},{10,... | collective-permute-start | bytes 884744 | tf_op jit(solution)/shard_map/ppermute | solution.py:434
  228.9 43.6 %collective-permute-start.49 = (bf16[768,768]{1,0:T(8,128)(2,1)S(1)}, bf16[768,768]{1,0:T(8,128)(2,1)S(1)}, u32[]{:S(2)}, u32[]{:S(2)}) collective-permute-start(bf16[768,768]{1,0:T(8,128)(2,1)S(1)} %add_convert_fusion.1), channel_id=1, source_target_pairs={{0,2},{1,3},{2,0},{3,1},{4,6},{5,7},{6,4},{7,5},{8,10},{9,11},{10,... | collective-permute-start | bytes 3538952 | tf_op jit(solution)/shard_map/ppermute | solution.py:434
  239.0 29.1 %collective-permute-start.25 = (bf16[192,768]{1,0:T(8,128)(2,1)S(1)}, bf16[192,768]{1,0:T(8,128)(2,1)S(1)}, u32[]{:S(2)}, u32[]{:S(2)}) collective-permute-start(bf16[192,768]{1,0:T(8,128)(2,1)S(1)} %get-tuple-element.95), channel_id=1, source_target_pairs={{0,2},{1,3},{2,0},{3,1},{4,6},{5,7},{6,4},{7,5},{8,10},{9,11},{10,... | collective-permute-start | bytes 884744 | tf_op jit(solution)/shard_map/ppermute | solution.py:434
  252.7 16.6 %collective-permute-start.26 = (bf16[192,768]{1,0:T(8,128)(2,1)S(1)}, bf16[192,768]{1,0:T(8,128)(2,1)S(1)}, u32[]{:S(2)}, u32[]{:S(2)}) collective-permute-start(bf16[192,768]{1,0:T(8,128)(2,1)S(1)} %get-tuple-element.94), channel_id=1, source_target_pairs={{0,6},{1,7},{2,4},{3,5},{4,2},{5,3},{6,0},{7,1},{8,14},{9,15},{10,... | collective-permute-start | bytes 884744 | tf_op jit(solution)/shard_map/ppermute | solution.py:434
  268.1 9.3 %collective-permute-start.20 = (bf16[2,192,384]{2,1,0:T(8,128)(2,1)S(1)}, bf16[2,192,384]{2,1,0:T(8,128)(2,1)S(1)}, u32[]{:S(2)}, u32[]{:S(2)}) collective-permute-start(bf16[2,192,384]{2,1,0:T(8,128)(2,1)S(1)} %add_convert_fusion.15), channel_id=1, source_target_pairs={{0,4},{1,5},{2,6},{3,7},{4,0},{5,1},{6,2},{7,3},{8,12},{9,13},{10,... | collective-permute-start | bytes 884744 | tf_op jit(solution)/shard_map/ppermute | solution.py:434
  269.4 7.8 %collective-permute-start.27 = (bf16[192,768]{1,0:T(8,128)(2,1)S(1)}, bf16[192,768]{1,0:T(8,128)(2,1)S(1)}, u32[]{:S(2)}, u32[]{:S(2)}) collective-permute-start(bf16[192,768]{1,0:T(8,128)(2,1)S(1)} %add_convert_fusion.14), channel_id=1, source_target_pairs={{0,8},{1,9},{2,10},{3,11},{4,12},{5,13},{6,14},{7,15},{8,0},{9,1},... | collective-permute-start | bytes 884744 | tf_op jit(solution)/shard_map/ppermute | solution.py:434
  271.6 20.0 %collective-permute-start.41 = (bf16[384,768]{1,0:T(8,128)(2,1)S(1)}, bf16[384,768]{1,0:T(8,128)(2,1)S(1)}, u32[]{:S(2)}, u32[]{:S(2)}) collective-permute-start(bf16[384,768]{1,0:T(8,128)(2,1)S(1)} %slice_bitcast_fusion), channel_id=1, source_target_pairs={{0,2},{1,3},{2,0},{3,1},{4,6},{5,7},{6,4},{7,5},{8,10},{9,11},{10,... | collective-permute-start | bytes 1769480 | tf_op jit(solution)/shard_map/ppermute | solution.py:434
  273.4 19.8 %collective-permute-start.50 = (bf16[384,768]{1,0:T(8,128)(2,1)S(1)}, bf16[384,768]{1,0:T(8,128)(2,1)S(1)}, u32[]{:S(2)}, u32[]{:S(2)}) collective-permute-start(bf16[384,768]{1,0:T(8,128)(2,1)S(1)} %constant_dynamic-slice_fusion.2), channel_id=1, source_target_pairs={{0,4},{1,5},{2,6},{3,7},{4,0},{5,1},{6,2},{7,3},{8,12},{9,13},{10,... | collective-permute-start | bytes 1769480 | tf_op jit(solution)/shard_map/ppermute | solution.py:434
  277.3 12.1 %collective-permute-start.28 = (bf16[192,768]{1,0:T(8,128)(2,1)S(1)}, bf16[192,768]{1,0:T(8,128)(2,1)S(1)}, u32[]{:S(2)}, u32[]{:S(2)}) collective-permute-start(bf16[192,768]{1,0:T(8,128)(2,1)S(1)} %add_convert_fusion.13), channel_id=1, source_target_pairs={{0,16},{1,17},{2,18},{3,19},{4,20},{5,21},{6,22},{7,23},{8,24},{9,... | collective-permute-start | bytes 884744 | tf_op jit(solution)/shard_map/ppermute | solution.py:434
  277.5 29.0 %collective-permute-start.21 = (bf16[2,384,384]{2,1,0:T(8,128)(2,1)S(1)}, bf16[2,384,384]{2,1,0:T(8,128)(2,1)S(1)}, u32[]{:S(2)}, u32[]{:S(2)}) collective-permute-start(bf16[2,384,384]{2,1,0:T(8,128)(2,1)S(1)} %pad_maximum_fusion.2), channel_id=1, source_target_pairs={{0,2},{1,3},{2,0},{3,1},{4,6},{5,7},{6,4},{7,5},{8,10},{9,11},{10,... | collective-permute-start | bytes 1769480 | tf_op jit(solution)/shard_map/ppermute | solution.py:434
  289.5 17.7 %collective-permute-start.29 = (bf16[192,768]{1,0:T(8,128)(2,1)S(1)}, bf16[192,768]{1,0:T(8,128)(2,1)S(1)}, u32[]{:S(2)}, u32[]{:S(2)}) collective-permute-start(bf16[192,768]{1,0:T(8,128)(2,1)S(1)} %add_convert_fusion.12), channel_id=1, source_target_pairs={{0,6},{1,7},{2,4},{3,5},{4,2},{5,3},{6,0},{7,1},{8,14},{9,15},{10,... | collective-permute-start | bytes 884744 | tf_op jit(solution)/shard_map/ppermute | solution.py:434
  290.4 19.3 %collective-permute-start.30 = (bf16[192,768]{1,0:T(8,128)(2,1)S(1)}, bf16[192,768]{1,0:T(8,128)(2,1)S(1)}, u32[]{:S(2)}, u32[]{:S(2)}) collective-permute-start(bf16[192,768]{1,0:T(8,128)(2,1)S(1)} %add_convert_fusion.12), channel_id=1, source_target_pairs={{0,2},{1,3},{2,0},{3,1},{4,6},{5,7},{6,4},{7,5},{8,10},{9,11},{10,... | collective-permute-start | bytes 884744 | tf_op jit(solution)/shard_map/ppermute | solution.py:434
  291.6 18.1 %collective-permute-start.31 = (bf16[192,768]{1,0:T(8,128)(2,1)S(1)}, bf16[192,768]{1,0:T(8,128)(2,1)S(1)}, u32[]{:S(2)}, u32[]{:S(2)}) collective-permute-start(bf16[192,768]{1,0:T(8,128)(2,1)S(1)} %add_convert_fusion.12), channel_id=1, source_target_pairs={{0,4},{1,5},{2,6},{3,7},{4,0},{5,1},{6,2},{7,3},{8,12},{9,13},{10,... | collective-permute-start | bytes 884744 | tf_op jit(solution)/shard_map/ppermute | solution.py:434
  293.2 16.7 %collective-permute-start.42 = (bf16[192,768]{1,0:T(8,128)(2,1)S(1)}, bf16[192,768]{1,0:T(8,128)(2,1)S(1)}, u32[]{:S(2)}, u32[]{:S(2)}) collective-permute-start(bf16[192,768]{1,0:T(8,128)(2,1)S(1)} %constant_dynamic-slice_fusion.5), channel_id=1, source_target_pairs={{0,8},{1,9},{2,10},{3,11},{4,12},{5,13},{6,14},{7,15},{8,0},{9,1},... | collective-permute-start | bytes 884744 | tf_op jit(solution)/shard_map/ppermute | solution.py:434
  307.2 45.9 %collective-permute-start.22 = (bf16[2,768,384]{2,1,0:T(8,128)(2,1)S(1)}, bf16[2,768,384]{2,1,0:T(8,128)(2,1)S(1)}, u32[]{:S(2)}, u32[]{:S(2)}) collective-permute-start(bf16[2,768,384]{2,1,0:T(8,128)(2,1)S(1)} %pad_maximum_fusion), channel_id=1, source_target_pairs={{0,1},{1,0},{2,3},{3,2},{4,5},{5,4},{6,7},{7,6},{8,9},{9,8},{10,11... | collective-permute-start | bytes 3538952 | tf_op jit(solution)/shard_map/ppermute | solution.py:434
  309.9 47.1 %collective-permute-start.32 = (bf16[768,768]{1,0:T(8,128)(2,1)S(1)}, bf16[768,768]{1,0:T(8,128)(2,1)S(1)}, u32[]{:S(2)}, u32[]{:S(2)}) collective-permute-start(bf16[768,768]{1,0:T(8,128)(2,1)S(1)} %pad_maximum_fusion.1), channel_id=1, source_target_pairs={{0,1},{1,0},{2,3},{3,2},{4,5},{5,4},{6,7},{7,6},{8,9},{9,8},{10,11... | collective-permute-start | bytes 3538952 | tf_op jit(solution)/shard_map/ppermute | solution.py:434
  310.1 13.3 %collective-permute-start.43 = (bf16[96,768]{1,0:T(8,128)(2,1)S(1)}, bf16[96,768]{1,0:T(8,128)(2,1)S(1)}, u32[]{:S(2)}, u32[]{:S(2)}) collective-permute-start(bf16[96,768]{1,0:T(8,128)(2,1)S(1)} %constant_dynamic-slice_fusion.4), channel_id=1, source_target_pairs={{0,16},{1,17},{2,18},{3,19},{4,20},{5,21},{6,22},{7,23},{8,24},{9,... | collective-permute-start | bytes 442376 | tf_op jit(solution)/shard_map/ppermute | solution.py:434
  313.4 19.5 %collective-permute-start.52 = (bf16[96,768]{1,0:T(8,128)(2,1)S(1)}, bf16[96,768]{1,0:T(8,128)(2,1)S(1)}, u32[]{:S(2)}, u32[]{:S(2)}) collective-permute-start(bf16[96,768]{1,0:T(8,128)(2,1)S(1)} %constant_dynamic-slice_fusion), channel_id=1, source_target_pairs={{0,16},{1,17},{2,18},{3,19},{4,20},{5,21},{6,22},{7,23},{8,24},{9,... | collective-permute-start | bytes 442376 | tf_op jit(solution)/shard_map/ppermute | solution.py:434
  323.4 12.6 %collective-permute-start.44 = (bf16[96,768]{1,0:T(8,128)(2,1)S(1)}, bf16[96,768]{1,0:T(8,128)(2,1)S(1)}, u32[]{:S(2)}, u32[]{:S(2)}) collective-permute-start(bf16[96,768]{1,0:T(8,128)(2,1)S(1)} %add_convert_fusion.19), channel_id=1, source_target_pairs={{0,16},{1,17},{2,18},{3,19},{4,20},{5,21},{6,22},{7,23},{8,24},{9,... | collective-permute-start | bytes 442376 | tf_op jit(solution)/shard_map/ppermute | solution.py:434
  332.9 6.8 %collective-permute-start.53 = (bf16[96,768]{1,0:T(8,128)(2,1)S(1)}, bf16[96,768]{1,0:T(8,128)(2,1)S(1)}, u32[]{:S(2)}, u32[]{:S(2)}) collective-permute-start(bf16[96,768]{1,0:T(8,128)(2,1)S(1)} %add_convert_fusion.18), channel_id=1, source_target_pairs={{0,16},{1,17},{2,18},{3,19},{4,20},{5,21},{6,22},{7,23},{8,24},{9,... | collective-permute-start | bytes 442376 | tf_op jit(solution)/shard_map/ppermute | solution.py:434
  336.1 10.0 %collective-permute-start.45 = (bf16[192,768]{1,0:T(8,128)(2,1)S(1)}, bf16[192,768]{1,0:T(8,128)(2,1)S(1)}, u32[]{:S(2)}, u32[]{:S(2)}) collective-permute-start(bf16[192,768]{1,0:T(8,128)(2,1)S(1)} %pad_maximum_fusion.5), channel_id=1, source_target_pairs={{0,8},{1,9},{2,10},{3,11},{4,12},{5,13},{6,14},{7,15},{8,0},{9,1},... | collective-permute-start | bytes 884744 | tf_op jit(solution)/shard_map/ppermute | solution.py:434
  339.8 12.5 %collective-permute-start.54 = (bf16[192,768]{1,0:T(8,128)(2,1)S(1)}, bf16[192,768]{1,0:T(8,128)(2,1)S(1)}, u32[]{:S(2)}, u32[]{:S(2)}) collective-permute-start(bf16[192,768]{1,0:T(8,128)(2,1)S(1)} %pad_maximum_fusion.6), channel_id=1, source_target_pairs={{0,8},{1,9},{2,10},{3,11},{4,12},{5,13},{6,14},{7,15},{8,0},{9,1},... | collective-permute-start | bytes 884744 | tf_op jit(solution)/shard_map/ppermute | solution.py:434
  346.5 16.3 %collective-permute-start.46 = (bf16[384,768]{1,0:T(8,128)(2,1)S(1)}, bf16[384,768]{1,0:T(8,128)(2,1)S(1)}, u32[]{:S(2)}, u32[]{:S(2)}) collective-permute-start(bf16[384,768]{1,0:T(8,128)(2,1)S(1)} %pad_maximum_fusion.3), channel_id=1, source_target_pairs={{0,4},{1,5},{2,6},{3,7},{4,0},{5,1},{6,2},{7,3},{8,12},{9,13},{10,... | collective-permute-start | bytes 1769480 | tf_op jit(solution)/shard_map/ppermute | solution.py:434
  352.5 21.9 %collective-permute-start.55 = (bf16[384,768]{1,0:T(8,128)(2,1)S(1)}, bf16[384,768]{1,0:T(8,128)(2,1)S(1)}, u32[]{:S(2)}, u32[]{:S(2)}) collective-permute-start(bf16[384,768]{1,0:T(8,128)(2,1)S(1)} %pad_maximum_fusion.4), channel_id=1, source_target_pairs={{0,4},{1,5},{2,6},{3,7},{4,0},{5,1},{6,2},{7,3},{8,12},{9,13},{10,... | collective-permute-start | bytes 1769480 | tf_op jit(solution)/shard_map/ppermute | solution.py:434
  (70 other events, 268.8 us)
